TPU v7x, 32 devices: a whole 2x2x4 slice. The times are simulated.
32 devices in a mesh: dp: 16 (over z, y, x), head: 2 (over core).
Axes of the slice: x: 2, y: 2, z: 4, core: 2. Of those that a mesh axis runs over, the one named last changes fastest.
Arguments:
- inputs: bfloat16 [16384, 1280], P(('dp', 'head')), may hold values from -6 to 6
- segment_ids: int32 [32, 512], P(('dp', 'head')), may hold values from 0 to 3, never falling along the last dimension, each value on 1 to 256 neighbouring positions
- gain_attn: float32 [1280], replicated, may hold values from 0.1 to 1.9
- w_qkv: bfloat16 [1280, 3840], replicated, may hold values from -0.15625 to 0.15625
- w_out: bfloat16 [1280, 1280], replicated, may hold values from -1 to 1
- gain_mlp: float32 [1280], replicated, may hold values from 0.1 to 1.9
- w_up: bfloat16 [1280, 5120], replicated, may hold values from -0.15625 to 0.15625
- w_down: bfloat16 [5120, 1280], replicated, may hold values from -0.078125 to 0.078125
- gain_final: float32 [1280], replicated, may hold values from 0.1 to 1.9
- head_projection_weight: bfloat16 [1280, 1280], P(None, 'head'), may hold values from -0.15625 to 0.15625
- head_output_bias: float32 [1280], P('head'), may hold values from -5 to 5
- cotangent: bfloat16 [16384, 1280], P('dp', 'head'), may hold values from -6 to 6
Outputs:
- predicted_levels: float32 [16384, 1280], P('dp', 'head')
- entry_sensitivity_matrix: float32 [16384, 1280], P(('dp', 'head'))
- grad_gain_attn: float32 [1280], P(('dp', 'head'))
- grad_qkv: float32 [1280, 3840], P(('dp', 'head'))
- grad_out: float32 [1280, 1280], P(('dp', 'head'))
- grad_gain_mlp: float32 [1280], P(('dp', 'head'))
- grad_up: float32 [1280, 5120], P(('dp', 'head'))
- grad_down: float32 [5120, 1280], P(('dp', 'head'))
- grad_gain_final: float32 [1280], P(('dp', 'head'))
- grad_head: float32 [1280, 1280], P('dp', 'head')
- grad_bias: float32 [1280], P('head')
Inputs may be any that keep to these rules, and one draw needn't show every extreme that they name: `segment_ids`: in each row the series ids never fall; each series spans 1 to 256 tokens, and in every row one spans exactly 256.
All inputs are finite; a program needn't handle non-finite values.
Results may differ from a plain program's by a relative error of at most 0.017.
Values may be sent and summed in bfloat16 or wider, within the bound.
A program may use at most 320 MiB of HBM per device.

v0:
```python
import functools
import math

import jax
import jax.numpy as jnp
import numpy as np
from jax import lax
from jax.experimental import pallas as pl
from jax.experimental.pallas import tpu as pltpu
from jax.sharding import PartitionSpec as P

HEADS = 16
F32 = jnp.float32
BF16 = jnp.bfloat16

epsilon = 1e-06


def rms_forward(values, gain):
    inverse = lax.rsqrt(jnp.mean(values * values, axis=-1, keepdims=True) + epsilon)
    return (values * inverse * gain, inverse)


def rms_backward(values, inverse, gain, grad):
    normed = values * inverse
    scaled = grad * gain
    grad_gain = jnp.sum(grad * normed, axis=0)
    grad_values = inverse * (scaled - normed * jnp.mean(scaled * normed, axis=-1, keepdims=True))
    return (grad_values, grad_gain)


def rotary_tables(sequence_span, hdim):
    half = hdim // 2
    freq = 10000.0 ** (-jnp.arange(half, dtype=jnp.float32) / half)
    angle = jnp.arange(sequence_span, dtype=jnp.float32)[:, None] * freq[None, :]
    return (jnp.cos(angle)[:, None, :], jnp.sin(angle)[:, None, :])


def rotate(values, cosine, sine):
    half = values.shape[-1] // 2
    first = values[..., :half]
    second = values[..., half:]
    return jnp.concatenate(
        [first * cosine - second * sine, second * cosine + first * sine], axis=-1
    )


def unrotate(grads, cosine, sine):
    half = grads.shape[-1] // 2
    first = grads[..., :half]
    second = grads[..., half:]
    return jnp.concatenate(
        [first * cosine + second * sine, second * cosine - first * sine], axis=-1
    )


def allowed_mask(segs):
    place = jnp.arange(segs.shape[0])
    return (segs[:, None] == segs[None, :]) & (place[:, None] >= place[None, :])


def row_scores(query, key, segs, scale):
    scores = jnp.einsum("qhd,khd->hqk", query, key, preferred_element_type=jnp.float32) * scale
    allowed = allowed_mask(segs)[None]
    return (jnp.where(allowed, scores, -1e30), allowed)


def attend_forward(items, scale):
    query, key, value, segs = items
    scores, allowed = row_scores(query, key, segs, scale)
    peak = jnp.max(scores, axis=-1, keepdims=True)
    expo = jnp.exp(scores - peak)
    overall_number = jnp.sum(expo, axis=-1, keepdims=True)
    probs = (expo / overall_number).astype(jnp.bfloat16)
    attended = jnp.einsum("hqk,khd->qhd", probs, value, preferred_element_type=jnp.float32)
    return (attended.astype(jnp.bfloat16), peak + jnp.log(overall_number))


def attend_backward(items, scale):
    query, key, value, segs, log_total, grad_attended = items
    scores, allowed = row_scores(query, key, segs, scale)
    probs = jnp.where(allowed, jnp.exp(scores - log_total), 0.0)
    grad_value = jnp.einsum(
        "hqk,qhd->khd",
        probs.astype(jnp.bfloat16),
        grad_attended,
        preferred_element_type=jnp.float32,
    )
    grad_probs = jnp.einsum(
        "qhd,khd->hqk", grad_attended, value, preferred_element_type=jnp.float32
    )
    grad_scores = (
        probs * (grad_probs - jnp.sum(grad_probs * probs, axis=-1, keepdims=True))
    ).astype(jnp.bfloat16)
    grad_query = (
        jnp.einsum("hqk,khd->qhd", grad_scores, key, preferred_element_type=jnp.float32) * scale
    )
    grad_key = (
        jnp.einsum("hqk,qhd->khd", grad_scores, query, preferred_element_type=jnp.float32) * scale
    )
    return (grad_query, grad_key, grad_value)


def contract_rows(left, right):
    return lax.dot_general(
        left, right, (((0,), (0,)), ((), ())), preferred_element_type=jnp.float32
    )


def contract_cols(left, right):
    return lax.dot_general(
        left, right, (((1,), (1,)), ((), ())), preferred_element_type=jnp.float32
    )


def swap_cores(values):
    return lax.ppermute(values, "head", [(0, 1), (1, 0)])


def flip(values, bit):
    size = lax.axis_size("dp")
    return lax.ppermute(values, "dp", [(i, i ^ bit) for i in range(size)])


def scatter_rows(left, right):
    return lax.psum_scatter(
        contract_rows(left, right), ("dp", "head"), scatter_dimension=0, tiled=True
    )


def sum_everywhere(values, over_head):
    size = lax.axis_size("dp")
    if over_head:
        values = values + swap_cores(values)
    bit = 1
    while bit < size:
        values = values + flip(values, bit)
        bit *= 2
    return values


MESH = pl.DeviceIdType.MESH


def chunk_table(width, hidden):
    table = [(0, 0)]
    table += [(1, j) for j in range(hidden // width)]
    table += [(2, j) for j in range(hidden // width)]
    table += [(3, 0)]
    table += [(4, j) for j in range(3)]
    return table


def nt(left, right):
    return lax.dot_general(
        left, right, (((1,), (1,)), ((), ())), preferred_element_type=jnp.float32
    )


def nn(left, right):
    return jnp.dot(left, right, preferred_element_type=jnp.float32)


def tt(left, right):
    return lax.dot_general(
        left, right, (((0,), (0,)), ((), ())), preferred_element_type=jnp.float32
    )


def columns_of(rows, scratch):
    scratch[...] = jnp.zeros_like(scratch)
    for i, row in enumerate(rows):
        scratch[i : i + 1] = row[...].reshape(1, row.shape[0])
    return scratch[...].T


def mask_of(seg_row, bias):
    tokens = bias.shape[0]
    ids = seg_row[...].astype(F32)
    wide = jnp.broadcast_to(ids, (8, tokens)).T[:, :1]
    own = lax.broadcasted_iota(jnp.int32, (tokens, tokens), 0)
    asked = lax.broadcasted_iota(jnp.int32, (tokens, tokens), 1)
    bias[...] = jnp.where((wide == ids) & (own <= asked), 0.0, -1e30)


STRIP = 128
SLOTS = 4
REACH = 256
TOGETHER = 2


def query_blocks(tokens):
    for start in range(0, tokens, REACH):
        stop = min(start + REACH, tokens)
        yield max(0, start - REACH), stop, slice(start, stop)


def norm_backward(vref, eref, gains, index, emit):
    width, tokens = vref.shape

    def sums_of(k, carry):
        squares, products = carry
        rows = pl.ds(pl.multiple_of(k * STRIP, STRIP), STRIP)
        v = vref[rows].astype(F32)
        e = eref[rows]
        gain = gains[rows, index : index + 1]
        squares = squares + jnp.sum(v * v, axis=0, keepdims=True)
        products = products + jnp.sum(e * gain * v, axis=0, keepdims=True)
        return squares, products

    blank = jnp.zeros((1, tokens), F32)
    squares, products = lax.fori_loop(0, width // STRIP, sums_of, (blank, blank))
    inverse = lax.rsqrt(squares / width + epsilon)
    mean = products * inverse / width

    @pl.loop(0, width // STRIP)
    def _(k):
        rows = pl.ds(pl.multiple_of(k * STRIP, STRIP), STRIP)
        normed = vref[rows].astype(F32) * inverse
        e = eref[rows]
        gain = gains[rows, index : index + 1]
        gains[rows, 8 + index : 9 + index] = jnp.sum(e * normed, axis=1, keepdims=True)
        emit(k, rows, inverse * (e * gain - normed * mean))


def forward_kernel(
    x,
    w_qkv,
    w_out,
    w_up,
    w_down,
    w_head,
    cot,
    seg_row,
    gain_attn,
    gain_mlp,
    gain_final,
    cosine,
    sine,
    y_t,
    g_t,
    a2_t,
    o_t,
    a1_t,
    y_o,
    g_o,
    a2_o,
    o_o,
    a1_o,
    dx3_t,
    e3_t,
    gain_columns,
    x2_t,
    x_t,
    h_t,
    qkv_t,
    lse,
    weights,
    xin,
    xt,
    act1,
    act2,
    final,
    mixed,
    qkv,
    res2,
    res3,
    hbuf,
    gbuf,
    bias,
    gains,
    gain_rows,
    cbuf,
    head_weight,
    dy,
    dy_sent,
    dy_got,
    e3,
    weight_sem,
    in_sem,
    c_sem,
    out_sem,
    h_sem,
    g_sem,
    push_send,
    push_recv,
    g_send,
    g_recv,
):
    width, tokens = res2.shape
    hidden = h_t.shape[0]
    pieces = hidden // width
    half = width // 2
    count = HEADS
    hdim = width // count
    scale = 1.0 / math.sqrt(hdim)
    first_tiles = [w_qkv.at[:, k * width : (k + 1) * width] for k in range(3)] + [w_out]

    def fetch(k):
        return pltpu.make_async_copy(first_tiles[k], weights.at[k], weight_sem.at[k])

    def fetch_up(k):
        slot = lax.rem(2 * k, SLOTS)
        source = w_up.at[:, pl.ds(pl.multiple_of(k * width, 128), width)]
        return pltpu.make_async_copy(source, weights.at[slot], weight_sem.at[slot])

    def fetch_down(k):
        slot = lax.rem(2 * k + 1, SLOTS)
        source = w_down.at[pl.ds(pl.multiple_of(k * width, 16), width)]
        return pltpu.make_async_copy(source, weights.at[slot], weight_sem.at[slot])

    me = lax.axis_index("dp")
    core = lax.axis_index("head")
    other = 1 - core

    def remote(src, dst, send, recv):
        return pltpu.make_async_remote_copy(
            src_ref=src,
            dst_ref=dst,
            send_sem=send,
            recv_sem=recv,
            device_id=(me, other),
            device_id_type=MESH,
        )

    fetch_head_weight = pltpu.make_async_copy(w_head, head_weight, c_sem.at[2])

    def fetch_c(number, which):
        start = pl.multiple_of(which * tokens, 16)
        return pltpu.make_async_copy(
            cot.at[pl.ds(start, tokens)], cbuf.at[number], c_sem.at[number]
        )

    fetch_x = pltpu.make_async_copy(x, xin, in_sem)
    fetch_x.start()
    for k in range(SLOTS):
        fetch(k).start()
    fetch_c(1, other).start()
    fetch_head_weight.start()
    fetch_c(0, core).start()

    barrier = pltpu.get_barrier_semaphore()
    pl.semaphore_signal(barrier, inc=1, device_id=(me, other), device_id_type=MESH)
    gains[...] = jnp.zeros_like(gains)
    gains[:, :8] = columns_of((gain_attn, gain_mlp, gain_final), gain_rows)
    pl.semaphore_wait(barrier, 1)

    mask_of(seg_row, bias)
    fetch_x.wait()
    xt[...] = xin[...].T
    dy_push = remote(dy_sent, dy_got, push_send.at[0], push_recv.at[0])
    outs, pushes = [], [dy_push]

    def put(source, target, also=None):
        copy = pltpu.make_async_copy(source, target, out_sem.at[len(outs)])
        outs.append(copy)
        copy.start()
        if also is not None:
            number = len(pushes)
            pushes.append(remote(source, also, push_send.at[number], push_recv.at[number]))
            pushes[-1].start()

    put(xt, x_t)

    def squares_of(ref):
        def step(k, total):
            v = ref[pl.ds(pl.multiple_of(k * STRIP, STRIP), STRIP)].astype(F32)
            return total + jnp.sum(v * v, axis=0, keepdims=True)

        return lax.fori_loop(0, width // STRIP, step, jnp.zeros((1, tokens), F32))

    def normalize(ref, index, to):
        inverse = lax.rsqrt(squares_of(ref) / width + epsilon)

        @pl.loop(0, width // STRIP)
        def _(k):
            rows = pl.ds(pl.multiple_of(k * STRIP, STRIP), STRIP)
            to[rows] = (ref[rows].astype(F32) * inverse * gains[rows, index : index + 1]).astype(
                BF16
            )

    normalize(xt, 0, act1)
    put(act1, a1_t, a1_o)

    turn = hdim // 2
    for part in range(3):
        fetch(part).wait()

    @pl.loop(0, 2)
    def _(part):
        for lower in range(2):
            value = tt(weights[part, :, lower * half : (lower + 1) * half], act1[...])
            for head in range(count // 2):
                one = value[head * hdim : head * hdim + turn]
                two = value[head * hdim + turn : (head + 1) * hdim]
                turned = jnp.concatenate(
                    [one * cosine[...] - two * sine[...], two * cosine[...] + one * sine[...]],
                    axis=0,
                )
                base = pl.multiple_of(part * width + lower * half + head * hdim, 16)
                qkv[pl.ds(base, hdim)] = turned.astype(BF16)

    fetch_up(0).start()
    fetch_down(0).start()
    for lower in range(2):
        rows = slice(lower * half, (lower + 1) * half)
        value = tt(weights[2, :, rows], act1[...])
        qkv[2 * width + lower * half : 2 * width + (lower + 1) * half] = value.astype(BF16)
    fetch_up(1).start()
    put(qkv, qkv_t)

    def attend(head):
        def rows_of(part):
            return pl.ds(pl.multiple_of(part * width + head * hdim, 16), hdim)

        q_t = qkv[rows_of(0)]
        v_t = qkv[rows_of(2)]
        k = qkv[rows_of(1)].T
        for low, high, asked in query_blocks(tokens):
            scores = nn(k[low:high], q_t[:, asked]) * scale + bias[low:high, asked]
            peak = jnp.max(scores, axis=0, keepdims=True)
            expo = jnp.exp(scores - peak)
            amount = jnp.sum(expo, axis=0, keepdims=True)
            probs = (expo * (1.0 / amount)).astype(BF16)
            mixed[rows_of(0), asked] = nn(v_t[:, low:high], probs).astype(BF16)
            lse[head, :, asked] = peak + jnp.log(amount)

    @pl.loop(0, count // TOGETHER)
    def _(i):
        for u in range(TOGETHER):
            attend(i * TOGETHER + u)

    put(mixed, o_t, o_o)

    fetch_head_weight.wait()
    fetch_c(1, other).wait()
    for i in range(2):
        rows = slice(i * half, (i + 1) * half)
        dy_sent[rows] = nt(head_weight[rows], cbuf[1]).astype(BF16)
    dy_push.start()
    fetch_c(0, core).wait()
    for i in range(2):
        rows = slice(i * half, (i + 1) * half)
        dy[rows] = nt(head_weight[rows], cbuf[0])


    fetch(3).wait()
    for lower in range(2):
        rows = slice(lower * half, (lower + 1) * half)
        res2[rows] = xt[rows].astype(F32) + tt(weights[3, :, rows], mixed[...])
        res3[rows] = res2[rows]
    fetch_down(1).start()
    put(res2, x2_t)
    normalize(res2, 1, act2)
    put(act2, a2_t, a2_o)

    def piece(k):
        return pl.ds(pl.multiple_of(k * width, 16), width)

    def h_copy(k):
        slot = lax.rem(k, 2)
        return pltpu.make_async_copy(hbuf.at[slot], h_t.at[piece(k)], h_sem.at[slot])

    def g_copy(k):
        slot = lax.rem(k, 2)
        return pltpu.make_async_copy(gbuf.at[slot], g_t.at[piece(k)], g_sem.at[slot])

    def g_push(k):
        slot = lax.rem(k, 2)
        return remote(gbuf.at[slot], g_o.at[piece(k)], g_send.at[slot], g_recv.at[k])

    @pl.loop(0, pieces)
    def _(k):
        slot, up, down = lax.rem(k, 2), lax.rem(2 * k, SLOTS), lax.rem(2 * k + 1, SLOTS)
        fetch_up(k).wait()

        @pl.when(k >= 2)
        def _():
            h_copy(k - 2).wait()
            g_copy(k - 2).wait()
            g_push(k - 2).wait_send()

        for lower in range(2):
            rows = slice(lower * half, (lower + 1) * half)
            value = tt(weights[up, :, rows], act2[...])
            hbuf[slot, rows] = value.astype(BF16)
            gbuf[slot, rows] = (value / (1.0 + jnp.exp(-value))).astype(BF16)

        @pl.when(k + 2 < pieces)
        def _():
            fetch_up(k + 2).start()

        h_copy(k).start()
        g_copy(k).start()
        g_push(k).start()
        fetch_down(k).wait()
        for lower in range(2):
            rows = slice(lower * half, (lower + 1) * half)
            res3[rows] += tt(weights[down, :, rows], gbuf[slot])

        @pl.when(k + 2 < pieces)
        def _():
            fetch_down(k + 2).start()

    normalize(res3, 2, final)
    put(final, y_t, y_o)

    dy_push.wait_recv()

    @pl.loop(0, width // STRIP)
    def _(k):
        rows = pl.ds(pl.multiple_of(k * STRIP, STRIP), STRIP)
        dy[rows] = dy[rows] + dy_got[rows].astype(F32)

    def emit(k, rows, value):
        dy[rows] = value
        e3[rows] = value.astype(BF16)

    norm_backward(res3, dy, gains, 2, emit)
    put(dy, dx3_t)
    put(e3, e3_t)
    put(gains, gain_columns)
    for copy in outs:
        copy.wait()
    for k in range(max(0, pieces - 2), pieces):
        h_copy(k).wait()
        g_copy(k).wait()
        g_push(k).wait_send()
    for k in range(pieces):
        g_push(k).wait_recv()
    dy_push.wait_send()
    for push in pushes[1:]:
        push.wait()


def run_forward(x, w_qkv, w_out, w_up, w_down, w_head, cot, segs, gains, cosine, sine):
    tokens, width = x.shape
    hidden = w_up.shape[1]
    hdim = width // HEADS
    hbm = pl.BlockSpec(memory_space=pl.ANY)
    vmem = pl.BlockSpec(memory_space=pltpu.VMEM)
    flat = (width, tokens)
    shapes = [
        jax.ShapeDtypeStruct(shape, dtype)
        for shape, dtype in (
            (flat, BF16),
            ((hidden, tokens), BF16),
            (flat, BF16),
            (flat, BF16),
            (flat, BF16),
            (flat, BF16),
            ((hidden, tokens), BF16),
            (flat, BF16),
            (flat, BF16),
            (flat, BF16),
            (flat, F32),
            (flat, BF16),
            ((width, 128), F32),
            (flat, F32),
            (flat, BF16),
            ((hidden, tokens), BF16),
            ((3 * width, tokens), BF16),
            ((HEADS, 1, tokens), F32),
        )
    ]
    dma = pltpu.SemaphoreType.DMA
    return pl.pallas_call(
        forward_kernel,
        out_shape=shapes,
        in_specs=[hbm] * 7 + [vmem] * 6,
        out_specs=[hbm] * 17 + [vmem],
        scratch_shapes=[
            pltpu.VMEM((SLOTS, width, width), BF16),
            pltpu.VMEM((tokens, width), BF16),
            pltpu.VMEM(flat, BF16),
            pltpu.VMEM(flat, BF16),
            pltpu.VMEM(flat, BF16),
            pltpu.VMEM(flat, BF16),
            pltpu.VMEM(flat, BF16),
            pltpu.VMEM((3 * width, tokens), BF16),
            pltpu.VMEM(flat, F32),
            pltpu.VMEM(flat, F32),
            pltpu.VMEM((2,) + flat, BF16),
            pltpu.VMEM((2,) + flat, BF16),
            pltpu.VMEM((tokens, tokens), F32),
            pltpu.VMEM((width, 128), F32),
            pltpu.VMEM((8, width), F32),
            pltpu.VMEM((2, tokens, width // 2), BF16),
            pltpu.VMEM((width, width // 2), BF16),
            pltpu.VMEM(flat, F32),
            pltpu.VMEM(flat, BF16),
            pltpu.VMEM(flat, BF16),
            pltpu.VMEM(flat, BF16),
            dma((SLOTS,)),
            dma(()),
            dma((3,)),
            dma((10,)),
            dma((2,)),
            dma((2,)),
            dma((5,)),
            dma((5,)),
            dma((2,)),
            dma((hidden // width,)),
        ],
        compiler_params=pltpu.CompilerParams(
            collective_id=1, has_side_effects=True, vmem_limit_bytes=60 << 20
        ),
        name="forward",
    )(x, w_qkv, w_out, w_up, w_down, w_head, cot, segs, *gains, cosine, sine)


LEAD = 3


def backward_kernel(
    table,
    size,
    y_t,
    g_t,
    a2_t,
    o_t,
    a1_t,
    y_o,
    g_o,
    a2_o,
    o_o,
    a1_o,
    cot,
    dx3_t,
    e3_t,
    x2_t,
    x_t,
    h_t,
    qkv_t,
    gain_columns,
    w_down,
    w_up,
    w_out,
    w_qkv,
    lse,
    seg_row,
    cosine,
    sine,
    out_head,
    out_down,
    out_up,
    out_out,
    out_qkv,
    out_small,
    out_entry,
    e3_o,
    eh_o,
    e2_o,
    ep_o,
    eh_mine,
    lbuf,
    rbuf,
    cbuf,
    grad,
    recv1,
    pair,
    recv2,
    line,
    recv_up,
    recv_down,
    side,
    side_up,
    side_down,
    side1,
    side2,
    total,
    sums,
    sums_in,
    dx,
    work,
    acc,
    ebuf,
    bias,
    gains,
    wrows,
    wcols,
    hbuf,
    ehbuf,
    ep,
    eo,
    heads,
    obuf,
    push_send,
    push_recv,
    left_sem,
    right_sem,
    send1_sem,
    recv1_sem,
    send2_sem,
    recv2_sem,
    up_send,
    up_recv,
    down_send,
    down_recv,
    side_up_send,
    side_up_recv,
    side_down_send,
    side_down_recv,
    side1_send,
    side1_recv,
    side2_send,
    side2_recv,
    local_sem,
    swap_send,
    swap_recv,
    small_send,
    small_recv,
    row_sem,
    col_sem,
    h_sem,
    eh_out_sem,
    eh_in_sem,
    head_sem,
    fetch_sem,
    entry_sem,
):
    n = len(table)
    length = size // 4
    me = lax.axis_index("dp")
    core = lax.axis_index("head")
    other = 1 - core
    xi = lax.rem(me, 2)
    yi = lax.rem(me // 2, 2)
    zi = me // 4
    width, tokens = dx.shape
    hidden = h_t.shape[0]
    cols = width // 2
    block = width // size
    count, hdim = eo.shape[:2]
    scale = 1.0 / math.sqrt(hdim)
    flip_x = me + 1 - 2 * xi
    flip_y = me + 2 * (1 - 2 * yi)
    first_bit = jnp.where(core == 0, xi, yi)
    second_bit = jnp.where(core == 0, yi, xi)
    first_peer = jnp.where(core == 0, flip_x, flip_y)
    second_peer = jnp.where(core == 0, flip_y, flip_x)
    far = lax.rem(me + size // 2, size)
    near = me + 4 * (1 - 2 * lax.rem(zi, 2))
    rings = recv1.shape[0]
    ring2 = recv2.shape[0]
    ring_line = line.shape[0]
    ring_side, ring_in = side.shape[0], side1.shape[0]
    main = grad.shape[-1]

    fetch_dx = pltpu.make_async_copy(dx3_t, dx, fetch_sem.at[0])
    fetch_e3 = pltpu.make_async_copy(e3_t, ebuf, fetch_sem.at[1])
    fetch_gains = pltpu.make_async_copy(gain_columns, gains, fetch_sem.at[4])
    fetch_x2 = pltpu.make_async_copy(x2_t, work, fetch_sem.at[1])
    fetch_x = pltpu.make_async_copy(x_t, ebuf, fetch_sem.at[0])

    def local_c(half, which):
        start = pl.multiple_of(which * tokens, 16)
        return pltpu.make_async_copy(
            cot.at[pl.ds(start, tokens)], cbuf.at[half], fetch_sem.at[2 + half]
        )

    lefts = (y_t, g_t, a2_t, o_t, a1_t)
    left_others = (y_o, g_o, a2_o, o_o, a1_o)
    pieces = hidden // width

    def start_left(c):
        i, j = table[c]
        lower = pl.ds(j * block, block) if i == 1 else slice(None)
        for half, source in ((0, lefts[i]), (1, left_others[i])):
            pltpu.make_async_copy(
                source.at[:, lower, :], lbuf.at[c % 2, half], left_sem.at[c % 2, half]
            ).start()

    fetch_e3.start()
    start_left(0)
    local_c(0, core).start()
    local_c(1, other).start()
    start_left(1)
    fetch_dx.start()
    fetch_gains.start()

    barrier = pltpu.get_barrier_semaphore()
    for index, which in ((me, other), (flip_x, core), (flip_y, core), (far, core)):
        pl.semaphore_signal(barrier, inc=1, device_id=(index, which), device_id_type=MESH)

    @pl.when(zi > 0)
    def _():
        pl.semaphore_signal(barrier, inc=1, device_id=(me - 4, core), device_id_type=MESH)

    @pl.when(zi < length - 1)
    def _():
        pl.semaphore_signal(barrier, inc=1, device_id=(me + 4, core), device_id_type=MESH)

    inner = jnp.where(zi > 0, 1, 0) + jnp.where(zi < length - 1, 1, 0)
    pl.semaphore_wait(barrier, 4 + inner)

    def remote(src, dst, send, recv, index, which):
        return pltpu.make_async_remote_copy(
            src_ref=src,
            dst_ref=dst,
            send_sem=send,
            recv_sem=recv,
            device_id=(index, which),
            device_id_type=MESH,
        )

    PE3, PE2, PEP = range(3)

    def push(k):
        if k == PEP:
            wide = 3 * cols
            src, dst = ep.at[pl.ds(pl.multiple_of(other * wide, 16), wide)], ep_o
        else:
            src, dst = ebuf, (e3_o, e2_o)[k]
            src = src.at[pl.ds(pl.multiple_of(other * cols, 16), cols)]
        return remote(src, dst, push_send.at[k], push_recv.at[k], me, other)

    fetch_e3.wait()
    push(PE3).start()

    def start_right(c):
        i, j = table[c]
        slot = c % 2
        mine = pl.ds(pl.multiple_of(core * cols, 16), cols)
        rows = pl.ds(j * cols, cols)
        if i == 1:
            own, its = ebuf.at[mine], e3_o
            if j == 0:
                push(PE3).wait_recv()
        elif i == 2:
            own, its = eh_mine.at[rows], eh_o.at[rows]
            if j == 0:
                for piece in range(pieces):
                    eh_push(piece, 0).wait_recv()
        elif i == 3:
            own, its = ebuf.at[mine], e2_o
            push(PE2).wait_recv()
        else:
            start = pl.multiple_of(core * 3 * cols + j * cols, 16)
            own, its = ep.at[pl.ds(start, cols)], ep_o.at[rows]
            if j == 0:
                push(PEP).wait_recv()
        pltpu.make_async_copy(own, rbuf.at[slot, 0], right_sem.at[slot, 0]).start()
        pltpu.make_async_copy(its, rbuf.at[slot, 1], right_sem.at[slot, 1]).start()

    def eh_push(piece, slot):
        return remote(
            ehbuf.at[slot],
            eh_o.at[pl.ds(piece * cols, cols)],
            eh_out_sem.at[slot],
            eh_in_sem.at[piece],
            me,
            other,
        )

    def wait_left(slot):
        for half in range(2):
            pltpu.make_async_copy(
                lbuf.at[slot, half], lbuf.at[slot, half], left_sem.at[slot, half]
            ).wait()

    def wait_right(slot):
        for half in range(2):
            pltpu.make_async_copy(
                rbuf.at[slot, half], rbuf.at[slot, half], right_sem.at[slot, half]
            ).wait()

    def form(c, right, multiply):
        slot, ring, to = lax.rem(c, 2), lax.rem(c, LEAD), lax.rem(c, ring_side)

        for z in range(length):
            value = None
            for half in range(2):
                left = lbuf[slot, half, 4 * z : 4 * z + 4].reshape(4 * block, tokens)
                part = multiply(left, right[half])
                value = part if value is None else value + part
            value = value.astype(BF16)
            for q in range(4):
                x, y = q % 2, q // 2
                one = jnp.where(core == 0, x, y)
                two = jnp.where(core == 0, y, x)
                part = value[q * block : (q + 1) * block]
                grad[ring, one, two, z] = part[:, :main]
                side[to, z, one, two] = part[:, main:]
        send1(c).start()
        start_side(c, 1)

    def send1(c):
        ring, spot = lax.rem(c, LEAD), lax.rem(c, rings)
        return remote(
            grad.at[ring, 1 - first_bit],
            recv1.at[spot],
            send1_sem.at[ring],
            recv1_sem.at[spot],
            first_peer,
            core,
        )

    def send2(c):
        ring, spot = lax.rem(c, 2), lax.rem(c, ring2)
        return remote(
            pair.at[ring, 1 - second_bit],
            recv2.at[spot],
            send2_sem.at[ring],
            recv2_sem.at[spot],
            second_peer,
            core,
        )

    def send_up(c, step):
        ring, spot = lax.rem(c, ring_line), lax.rem(c, rings)
        return remote(
            line.at[ring, jnp.minimum(zi + (length - step), length - 1)],
            recv_up.at[spot, step - 1],
            up_send.at[ring, step - 1],
            up_recv.at[spot, step - 1],
            jnp.minimum(me + 4, size - 1),
            core,
        )

    def send_down(c, step):
        ring, spot = lax.rem(c, ring_line), lax.rem(c, rings)
        return remote(
            line.at[ring, jnp.maximum(zi - (length - step), 0)],
            recv_down.at[spot, step - 1],
            down_send.at[ring, step - 1],
            down_recv.at[spot, step - 1],
            jnp.maximum(me - 4, 0),
            core,
        )

    def side_send_up(c, step):
        ring, spot = lax.rem(c, ring_side), lax.rem(c, ring_in)
        return remote(
            side.at[ring, jnp.minimum(zi + (length - step), length - 1)],
            side_up.at[spot, step - 1],
            side_up_send.at[ring, step - 1],
            side_up_recv.at[spot, step - 1],
            jnp.minimum(me + 4, size - 1),
            core,
        )

    def side_send_down(c, step):
        ring, spot = lax.rem(c, ring_side), lax.rem(c, ring_in)
        return remote(
            side.at[ring, jnp.maximum(zi - (length - step), 0)],
            side_down.at[spot, step - 1],
            side_down_send.at[ring, step - 1],
            side_down_recv.at[spot, step - 1],
            jnp.maximum(me - 4, 0),
            core,
        )

    def side_send1(c):
        ring, spot = lax.rem(c, ring_side), lax.rem(c, ring_in)
        return remote(
            side.at[ring, zi, 1 - first_bit],
            side1.at[spot],
            side1_send.at[ring],
            side1_recv.at[spot],
            first_peer,
            core,
        )

    def side_send2(c):
        ring, spot = lax.rem(c, ring_side), lax.rem(c, ring_in)
        return remote(
            side.at[ring, zi, first_bit, 1 - second_bit],
            side2.at[spot],
            side2_send.at[ring],
            side2_recv.at[spot],
            second_peer,
            core,
        )

    def start_side(c, step):
        @pl.when(zi < step)
        def _():
            side_send_up(c, step).start()

        @pl.when(zi >= length - step)
        def _():
            side_send_down(c, step).start()

    def exchange_side(t):
        for step in range(1, length):

            @pl.when((t >= step - 1) & (t <= n + step - 2))
            def _():
                c = t - step + 1
                ring, at = lax.rem(c, ring_side), lax.rem(c, ring_in)
                up_in = (zi >= 1) & (zi <= step)
                down_in = (zi <= length - 2) & (zi >= length - 1 - step)

                @pl.when(up_in)
                def _():
                    side_send_up(c, step).wait_recv()
                    spot = jnp.minimum(zi + (length - 1 - step), length - 1)
                    side[ring, spot] = side[ring, spot] + side_up[at, step - 1]

                @pl.when(down_in)
                def _():
                    side_send_down(c, step).wait_recv()
                    spot = jnp.maximum(zi - (length - 1 - step), 0)
                    side[ring, spot] = side[ring, spot] + side_down[at, step - 1]

                if step < length - 1:
                    start_side(c, step + 1)
                else:
                    side_send1(c).start()

        @pl.when((t >= length - 1) & (t <= n + length - 2))
        def _():
            c = t - length + 1
            ring, at = lax.rem(c, ring_side), lax.rem(c, ring_in)
            side_send1(c).wait_recv()
            side[ring, zi, first_bit] = side[ring, zi, first_bit] + side1[at]
            side_send2(c).start()

        @pl.when((t >= length) & (t <= n + length - 1))
        def _():
            c = t - length
            ring, at = lax.rem(c, ring_side), lax.rem(c, ring_in)
            side_send2(c).wait_recv()
            total[c, :, main:] = side[ring, zi, first_bit, second_bit].astype(F32) + side2[
                at
            ].astype(F32)
            for back in range(1, length):

                @pl.when(zi < back)
                def _():
                    side_send_up(c, back).wait_send()

                @pl.when(zi >= length - back)
                def _():
                    side_send_down(c, back).wait_send()

            side_send1(c).wait_send()
            side_send2(c).wait_send()

    def start_line(c, step):
        @pl.when(zi < step)
        def _():
            send_up(c, step).start()

        @pl.when(zi >= length - step)
        def _():
            send_down(c, step).start()

    def wait_line_sent(c, step):
        @pl.when(zi < step)
        def _():
            send_up(c, step).wait_send()

        @pl.when(zi >= length - step)
        def _():
            send_down(c, step).wait_send()

    def results(c):
        i, j = table[c]
        if i == 0:
            return [pltpu.make_async_copy(total.at[c], out_head, local_sem.at[c])]
        if i == 1:
            target = out_down.at[
                pl.ds((j % 2) * block, block), pl.ds(pl.multiple_of(core * cols, 128), cols)
            ]
            return [
                pltpu.make_async_copy(total.at[c], target, local_sem.at[c]),
                remote(total.at[c], target, swap_send.at[c], swap_recv.at[c], me, other),
            ]
        target = (None, None, out_up, out_out, out_qkv)[i]
        wide = target.shape[1] // 2
        place = target.at[:, pl.ds(pl.multiple_of(core * wide + j * cols, 128), cols)]
        half = block // 2
        mine = pl.ds(pl.multiple_of(core * half, 8), half)
        its = pl.ds(pl.multiple_of(other * half, 8), half)
        return [
            pltpu.make_async_copy(total.at[c, mine], place, local_sem.at[c]),
            remote(total.at[c, its], place, swap_send.at[c], swap_recv.at[c], me, other),
        ]

    def start_results(c):
        i, j = table[c]
        copies = results(c)
        if i == 1:
            owner = j // (pieces // 2)
            pl.when(core == owner)(copies[0].start)
            pl.when(core != owner)(copies[1].start)
        else:
            for copy in copies:
                copy.start()

    def end_results(c):
        i, j = table[c]
        copies = results(c)
        if i == 1:
            owner = j // (pieces // 2)
            pl.when(core == owner)(copies[0].wait)
            pl.when(core == owner)(copies[1].wait_recv)
            pl.when(core != owner)(copies[1].wait_send)
        else:
            for copy in copies:
                copy.wait()

    def exchange(t):
        @pl.when(t < n)
        def _():
            c = t
            send1(c).wait_recv()
            ring, spot, to = lax.rem(c, LEAD), lax.rem(c, rings), lax.rem(c, 2)

            @pl.when(c >= 2)
            def _():
                send2(c - 2).wait_send()

            for two in range(2):

                @pl.loop(0, length)
                def _(z):
                    pair[to, two, z] = grad[ring, first_bit, two, z] + recv1[spot, two, z]

            send2(c).start()

        @pl.when((t >= 1) & (t <= n))
        def _():
            c = t - 1
            send2(c).wait_recv()
            ring, spot, to = lax.rem(c, 2), lax.rem(c, ring2), lax.rem(c, ring_line)

            @pl.loop(0, length)
            def _(z):
                line[to, z] = pair[ring, second_bit, z] + recv2[spot, z]

            start_line(c, 1)

        exchange_side(t)

        for step in range(1, length):

            @pl.when((t >= 1 + step) & (t <= n + step))
            def _():
                c = t - 1 - step
                ring, at = lax.rem(c, ring_line), lax.rem(c, rings)
                last = step == length - 1
                up_in = (zi >= 1) & (zi <= step)
                down_in = (zi <= length - 2) & (zi >= length - 1 - step)

                @pl.when(up_in)
                def _():
                    send_up(c, step).wait_recv()
                    spot = jnp.minimum(zi + (length - 1 - step), length - 1)
                    if not last:
                        line[ring, spot] = line[ring, spot] + recv_up[at, step - 1]

                @pl.when(down_in)
                def _():
                    send_down(c, step).wait_recv()
                    spot = jnp.maximum(zi - (length - 1 - step), 0)
                    if not last:
                        line[ring, spot] = line[ring, spot] + recv_down[at, step - 1]

                if not last:
                    start_line(c, step + 1)
                else:
                    total[c, :, :main] = line[ring, zi].astype(F32)

                    @pl.when(up_in)
                    def _():
                        total[c, :, :main] += recv_up[at, step - 1].astype(F32)

                    @pl.when(down_in)
                    def _():
                        total[c, :, :main] += recv_down[at, step - 1].astype(F32)

                    for back in range(1, length):
                        wait_line_sent(c, back)

                    for d in range(n):

                        @pl.when(c == d)
                        def _():
                            start_results(d)

    local_c(0, core).wait()
    local_c(1, other).wait()
    wait_left(0)
    form(0, [cbuf[0], cbuf[1]], nn)
    start_left(2)
    fetch_x2.start()
    sums[0] = jnp.zeros_like(sums[0])
    for i in range(2):
        share = jnp.sum(cbuf[i].astype(F32), axis=0, keepdims=True)
        at = pl.ds(pl.multiple_of(core * cols, 128), cols)
        sums[0, 3:4, at] = sums[0, 3:4, at] + share
    for c in range(1, LEAD):
        start_right(c)
        wait_left(c % 2)
        wait_right(c % 2)
        form(c, [rbuf[c % 2, 0], rbuf[c % 2, 1]], nt)
        start_left(c + 2)
    fetch_dx.wait()
    fetch_gains.wait()

    def row_tile(k, slot, source):
        return pltpu.make_async_copy(
            source.at[pl.ds(pl.multiple_of(k * cols, 16), cols)], wrows.at[slot], row_sem.at[slot]
        )

    def col_tile(k, slot, source):
        return pltpu.make_async_copy(
            source.at[:, pl.ds(pl.multiple_of(k * cols, 128), cols)],
            wcols.at[slot],
            col_sem.at[slot],
        )

    def h_tile(k, slot):
        return pltpu.make_async_copy(
            h_t.at[pl.ds(pl.multiple_of(k * cols, 16), cols)], hbuf.at[slot], h_sem.at[slot]
        )

    def mlp_tiles(k):
        return jnp.where(k < pieces, other, core) * pieces + lax.rem(k, pieces)

    def fetch_mlp(k):
        slot = lax.rem(k, 2)
        tile = mlp_tiles(k)
        row_tile(tile, slot, w_down).start()
        col_tile(tile, slot, w_up).start()
        h_tile(tile, slot).start()

    def mlp_step(k):
        slot = lax.rem(k, 2)
        tile = mlp_tiles(k)
        row_tile(tile, slot, w_down).wait()
        h_tile(tile, slot).wait()

        @pl.when((k >= 2) & (k < pieces + 2))
        def _():
            eh_push(0, slot).wait_send()

        @pl.when(k >= pieces + 2)
        def _():
            pltpu.make_async_copy(
                ehbuf.at[slot], eh_mine.at[pl.ds(0, cols)], eh_out_sem.at[slot]
            ).wait()

        part = cols // 2
        for i in range(2):
            rows = slice(i * part, (i + 1) * part)
            value = nn(wrows[slot, rows], ebuf[...])
            pre = hbuf[slot, rows].astype(F32)
            sig = 1.0 / (1.0 + jnp.exp(-pre))
            ehbuf[slot, rows] = (value * sig * (1.0 + pre * (1.0 - sig))).astype(BF16)

        where = lax.rem(k, pieces)

        @pl.when(k < pieces)
        def _():
            eh_push(where, slot).start()

        @pl.when(k >= pieces)
        def _():
            pltpu.make_async_copy(
                ehbuf.at[slot],
                eh_mine.at[pl.ds(pl.multiple_of(where * cols, 16), cols)],
                eh_out_sem.at[slot],
            ).start()

        col_tile(tile, slot, w_up).wait()
        accumulate(wcols.at[slot], ehbuf.at[slot], k == 0)

        @pl.when(k + 2 < 2 * pieces)
        def _():
            fetch_mlp(k + 2)

    def accumulate(left, right, first):
        @pl.when(first)
        def _():
            acc[...] = jnp.zeros_like(acc)

        part = width // 4
        for i in range(4):
            rows = slice(i * part, (i + 1) * part)
            acc[rows] += nn(left[rows], right[...])

    fetch_mlp(0)
    fetch_mlp(1)

    def emit_mlp(k, rows, value):
        value = dx[rows] + value
        dx[rows] = value
        ebuf[rows] = value.astype(BF16)

    def middle():
        for slot in range(2):
            pltpu.make_async_copy(
                ehbuf.at[slot], eh_mine.at[pl.ds(0, cols)], eh_out_sem.at[slot]
            ).wait()
        row_tile(0, 0, w_out).start()
        row_tile(1, 1, w_out).start()
        push(PE3).wait_send()
        fetch_x2.wait()
        norm_backward(work, acc, gains, 1, emit_mlp)
        push(PE2).start()

        @pl.loop(0, 2)
        def _(k):
            row_tile(k, k, w_out).wait()

            group = cols // hdim
            value = nn(wrows[k], ebuf[...]).astype(BF16)
            eo[pl.ds(k * group, group)] = value.reshape(group, hdim, tokens)

        mask_of(seg_row, bias)

    per_turn = count // 4

    def head_copy(head, slot, u, part):
        return pltpu.make_async_copy(
            qkv_t.at[pl.ds(pl.multiple_of(part * width + head * hdim, 16), hdim)],
            heads.at[slot, u, part],
            head_sem.at[slot, u, part],
        )

    def fetch_heads(i):
        for u in range(TOGETHER):
            for part in range(3):
                head_copy(i * TOGETHER + u, lax.rem(i, 2), u, part).start()

    def attend_head(head, slot, u):
        q_t, k_t, v_t = (heads[slot, u, part] for part in range(3))
        e_t = eo[head]
        q, k, v, e = q_t.T, k_t.T, v_t.T, e_t.T
        blocks = list(query_blocks(tokens))
        weight = lse[head]
        ek, ev, eqs = [[] for _ in blocks], [[] for _ in blocks], []
        for low, high, asked in blocks:
            scores = nn(k[low:high], q_t[:, asked]) * scale + bias[low:high, asked]
            p = jnp.exp(scores - weight[:, asked])
            ep_t = nn(v[low:high], e_t[:, asked])
            share = jnp.sum(p * ep_t, axis=0, keepdims=True)
            es = (p * (ep_t - share)).astype(BF16)
            eqs.append(nn(k_t[:, low:high], es))
            one, two = nn(es, q[asked]), nn(p.astype(BF16), e[asked])
            for number, (_, _, own) in enumerate(blocks):
                if low <= own.start < high:
                    ek[number].append(one[own.start - low : own.stop - low])
                    ev[number].append(two[own.start - low : own.stop - low])
        ek_t = jnp.concatenate([sum(terms[1:], terms[0]) for terms in ek], axis=0).T
        ev_t = jnp.concatenate([sum(terms[1:], terms[0]) for terms in ev], axis=0).T
        half = hdim // 2
        for part, value in ((0, jnp.concatenate(eqs, axis=1)), (1, ek_t)):
            one, two = value[:half] * scale, value[half:] * scale
            turned = jnp.concatenate(
                [one * cosine[...] + two * sine[...], two * cosine[...] - one * sine[...]],
                axis=0,
            )
            to = pl.ds(pl.multiple_of(part * width + head * hdim, 16), hdim)
            ep[to] = turned.astype(BF16)
        to = pl.ds(pl.multiple_of(2 * width + head * hdim, 16), hdim)
        ep[to] = ev_t.astype(BF16)

    def attend(turn):
        @pl.when(turn == 0)
        def _():
            fetch_heads(0)

        @pl.loop(0, per_turn // TOGETHER)
        def _(j):
            i = turn * (per_turn // TOGETHER) + j
            slot = lax.rem(i, 2)
            for u in range(TOGETHER):
                for part in range(3):
                    head_copy(i * TOGETHER + u, slot, u, part).wait()

            @pl.when((i + 1) * TOGETHER < count)
            def _():
                fetch_heads(i + 1)

            for u in range(TOGETHER):
                attend_head(i * TOGETHER + u, slot, u)

        @pl.when(turn == 3)
        def _():
            push(PEP).start()

    def fetch_qkv(k):
        col_tile(k, lax.rem(k, 2), w_qkv).start()

    def qkv_step(k):
        slot = lax.rem(k, 2)
        col_tile(k, slot, w_qkv).wait()
        rows = pl.ds(pl.multiple_of(k * cols, 16), cols)
        accumulate(wcols.at[slot], ep.at[rows], k == 0)

        @pl.when(k + 2 < 6)
        def _():
            fetch_qkv(k + 2)

    def entry_copy(k, slot):
        return pltpu.make_async_copy(
            obuf.at[slot],
            out_entry.at[:, pl.ds(pl.multiple_of(k * STRIP, STRIP), STRIP)],
            entry_sem.at[slot],
        )

    def emit_entry(k, rows, value):
        slot = lax.rem(k, 2)

        @pl.when(k >= 2)
        def _():
            entry_copy(k, slot).wait()

        obuf[slot] = (dx[rows] + value).T
        entry_copy(k, slot).start()

    peers = ((me, other), (flip_x, core), (flip_y, core), (near, core), (far, core))
    steps = len(peers)

    def small_copy(i):
        return remote(
            sums.at[i], sums_in.at[i], small_send.at[i], small_recv.at[i], peers[i][0], peers[i][1]
        )

    def last():
        fetch_x.wait()
        norm_backward(ebuf, acc, gains, 0, emit_entry)
        for slot in range(2):
            entry_copy(0, slot).wait()
        sums[0] = sums[0] + gains[...].T[8:16]
        small_copy(0).start()

    @pl.loop(0, n + length)
    def _(t):
        for c in range(LEAD, n):

            @pl.when(t == c - LEAD)
            def _():
                start_right(c)

        @pl.when(t < 2)
        def _():
            @pl.loop(0, pieces)
            def _(i):
                mlp_step(t * pieces + i)

        @pl.when(t == 2)
        def _():
            middle()

        @pl.when((t >= 3) & (t < 7))
        def _():
            attend(t - 3)

        @pl.when(t == 6)
        def _():
            fetch_qkv(0)
            fetch_qkv(1)

        @pl.when((t == 7) | (t == 8))
        def _():
            @pl.loop(0, 3)
            def _(i):
                qkv_step((t - 7) * 3 + i)

        @pl.when(t == 9)
        def _():
            last()

        for i in range(steps):

            @pl.when(t == 10 + i)
            def _():
                small_copy(i).wait()
                value = sums[i] + sums_in[i]
                if i == steps - 1:
                    out_small[...] = value
                else:
                    sums[i + 1] = value
                    small_copy(i + 1).start()

        exchange(t)

        @pl.when(t + LEAD < n)
        def _():
            c = t + LEAD
            slot = lax.rem(c, 2)
            wait_left(slot)
            wait_right(slot)
            send1(t).wait_send()
            form(c, [rbuf[slot, 0], rbuf[slot, 1]], nt)
            for d in range(LEAD + 2, n):

                @pl.when(c == d - 2)
                def _():
                    start_left(d)

        @pl.when(t == 8)
        def _():
            push(PE2).wait_send()
            fetch_x.start()

    for c in range(n):
        end_results(c)
    for c in range(n - LEAD, n):
        send1(c).wait_send()
    for c in range(n - 2, n):
        send2(c).wait_send()
    push(PEP).wait_send()


def run_backward(lefts, left_others, others, weights, tables):
    size = lax.axis_size("dp")
    width, tokens = lefts[0].shape
    hidden = lefts[1].shape[0]
    block = width // size
    cols = width // 2
    table = chunk_table(width, hidden)
    n = len(table)
    length = size // 4
    share = block // 2
    hdim = width // HEADS
    hbm = pl.BlockSpec(memory_space=pl.ANY)
    vmem = pl.BlockSpec(memory_space=pltpu.VMEM)
    lefts = [left.reshape(size, left.shape[0] // size, tokens) for left in lefts + left_others]
    shapes = [
        jax.ShapeDtypeStruct((block, cols), F32),
        jax.ShapeDtypeStruct((hidden // size // 2, width), F32),
        jax.ShapeDtypeStruct((share, hidden), F32),
        jax.ShapeDtypeStruct((share, width), F32),
        jax.ShapeDtypeStruct((share, 3 * width), F32),
        jax.ShapeDtypeStruct((8, width), F32),
        jax.ShapeDtypeStruct((tokens, width), F32),
    ]
    shapes += [
        jax.ShapeDtypeStruct((rows, tokens), BF16)
        for rows in (cols, hidden // 2, cols, 3 * cols, hidden // 2)
    ]
    dma = pltpu.SemaphoreType.DMA
    ring1, ring2, ring_line = 6, 4, length + 1
    main = cols - 128
    results = pl.pallas_call(
        functools.partial(backward_kernel, table, size),
        out_shape=shapes,
        in_specs=[hbm] * 22 + [vmem] * 4,
        out_specs=[hbm] * 5 + [vmem] + [hbm] * 6,
        scratch_shapes=[
            pltpu.VMEM((2, 2, size, block, tokens), BF16),
            pltpu.VMEM((2, 2, cols, tokens), BF16),
            pltpu.VMEM((2, tokens, cols), BF16),
            pltpu.VMEM((LEAD, 2, 2, length, block, main), BF16),
            pltpu.VMEM((ring1, 2, length, block, main), BF16),
            pltpu.VMEM((2, 2, length, block, main), BF16),
            pltpu.VMEM((ring2, length, block, main), BF16),
            pltpu.VMEM((ring_line, length, block, main), BF16),
            pltpu.VMEM((ring1, length - 1, block, main), BF16),
            pltpu.VMEM((ring1, length - 1, block, main), BF16),
            pltpu.VMEM((length + 4, length, 2, 2, block, cols - main), BF16),
            pltpu.VMEM((length + 3, length - 1, 2, 2, block, cols - main), BF16),
            pltpu.VMEM((length + 3, length - 1, 2, 2, block, cols - main), BF16),
            pltpu.VMEM((length + 3, 2, block, cols - main), BF16),
            pltpu.VMEM((length + 3, block, cols - main), BF16),
            pltpu.VMEM((n, block, cols), F32),
            pltpu.VMEM((5, 8, width), F32),
            pltpu.VMEM((5, 8, width), F32),
            pltpu.VMEM((width, tokens), F32),
            pltpu.VMEM((width, tokens), F32),
            pltpu.VMEM((width, tokens), F32),
            pltpu.VMEM((width, tokens), BF16),
            pltpu.VMEM((tokens, tokens), F32),
            pltpu.VMEM((width, 128), F32),
            pltpu.VMEM((2, cols, width), BF16),
            pltpu.VMEM((2, width, cols), BF16),
            pltpu.VMEM((2, cols, tokens), BF16),
            pltpu.VMEM((2, cols, tokens), BF16),
            pltpu.VMEM((3 * width, tokens), BF16),
            pltpu.VMEM((HEADS, hdim, tokens), BF16),
            pltpu.VMEM((2, TOGETHER, 3, hdim, tokens), BF16),
            pltpu.VMEM((2, tokens, 128), F32),
            dma((3,)),
            dma((3,)),
            dma((2, 2)),
            dma((2, 2)),
            dma((LEAD,)),
            dma((ring1,)),
            dma((2,)),
            dma((ring2,)),
            dma((ring_line, length - 1)),
            dma((ring1, length - 1)),
            dma((ring_line, length - 1)),
            dma((ring1, length - 1)),
            dma((length + 4, length - 1)),
            dma((length + 3, length - 1)),
            dma((length + 4, length - 1)),
            dma((length + 3, length - 1)),
            dma((length + 4,)),
            dma((length + 3,)),
            dma((length + 4,)),
            dma((length + 3,)),
            dma((n,)),
            dma((n,)),
            dma((n,)),
            dma((5,)),
            dma((5,)),
            dma((2,)),
            dma((2,)),
            dma((2,)),
            dma((2,)),
            dma((hidden // width,)),
            dma((2, TOGETHER, 3)),
            dma((5,)),
            dma((2,)),
        ],
        compiler_params=pltpu.CompilerParams(
            collective_id=0, has_side_effects=True, vmem_limit_bytes=62 << 20
        ),
        name="backward",
    )(*lefts, *others, *weights, *tables)
    return results[:7]


def finish_kernel(
    copied,
    *refs,
):
    sources = refs[:copied]
    sums, y_t, y_o, w_head, head_bias = refs[copied : copied + 5]
    results = refs[copied + 5 :]
    targets = results[:copied]
    levels, gain_attn, gain_mlp, gain_final, bias = results[copied : copied + 5]
    ybuf, wbuf, out, fetch_sem, copy_sem, in_sem, out_sem = results[copied + 5 : copied + 12]
    held = results[copied + 12 :]
    me = lax.axis_index("dp")
    core = lax.axis_index("head")
    width, tokens = y_t.shape
    half = width // 2
    fetches = [
        pltpu.make_async_copy(source, target, in_sem.at[i])
        for i, (source, target) in enumerate(
            ((w_head, wbuf), (y_t, ybuf.at[0]), (y_o, ybuf.at[1]))
        )
    ]
    for fetch in fetches:
        fetch.start()
    arrivals = [
        pltpu.make_async_copy(source, buffer, fetch_sem.at[i])
        for i, (source, buffer) in enumerate(zip(sources, held))
    ]
    copies = [
        pltpu.make_async_copy(buffer, target, copy_sem.at[i])
        for i, (buffer, target) in enumerate(zip(held, targets))
    ]
    for arrival in arrivals:
        arrival.start()
    share = gain_attn.shape[0]
    start = (me * 2 + core) * share
    rolled = pltpu.roll(sums[...], lax.rem(width - start, width), 1)
    for i, target in enumerate((gain_attn, gain_mlp, gain_final)):
        target[...] = rolled[i, :share]
    bias[...] = sums[3, pl.ds(pl.multiple_of(core * half, 128), half)]
    fetches[0].wait()
    part = tokens // 2

    def level_copy(i):
        which = core if i < 2 else 1 - core
        start = pl.multiple_of(which * tokens + (i % 2) * part, 8)
        return pltpu.make_async_copy(out.at[i], levels.at[pl.ds(start, part)], out_sem.at[i])

    for i in range(4):
        if i % 2 == 0:
            fetches[1 + i // 2].wait()
        at = slice((i % 2) * part, (i % 2 + 1) * part)
        out[i] = tt(ybuf[i // 2, :, at], wbuf[...]) + head_bias[...].reshape(1, half)
        level_copy(i).start()
        for k in range(i * len(copies) // 4, (i + 1) * len(copies) // 4):
            arrivals[k].wait()
            copies[k].start()
    for i in range(4):
        level_copy(i).wait()
    for copy in copies:
        copy.wait()


def run_finish(copied, sums, y_t, y_o, w_head, head_bias):
    width, tokens = y_t.shape
    half = width // 2
    share = width // (2 * lax.axis_size("dp"))
    hbm = pl.BlockSpec(memory_space=pl.ANY)
    vmem = pl.BlockSpec(memory_space=pltpu.VMEM)
    dma = pltpu.SemaphoreType.DMA
    shapes = [jax.ShapeDtypeStruct(value.shape, F32) for value in copied]
    shapes += [jax.ShapeDtypeStruct((2 * tokens, half), F32)]
    shapes += [jax.ShapeDtypeStruct((share,), F32)] * 3 + [jax.ShapeDtypeStruct((half,), F32)]
    return pl.pallas_call(
        functools.partial(finish_kernel, len(copied)),
        out_shape=shapes,
        in_specs=[hbm] * len(copied) + [vmem] + [hbm] * 3 + [vmem],
        out_specs=[hbm] * (len(copied) + 1) + [vmem] * 4,
        scratch_shapes=[
            pltpu.VMEM((2, width, tokens), BF16),
            pltpu.VMEM((width, half), BF16),
            pltpu.VMEM((4, tokens // 2, half), F32),
            dma((len(copied),)),
            dma((len(copied),)),
            dma((3,)),
            dma((4,)),
        ]
        + [pltpu.VMEM(value.shape, F32) for value in copied],
        compiler_params=pltpu.CompilerParams(vmem_limit_bytes=60 << 20),
        name="finish",
    )(*copied, sums, y_t, y_o, w_head, head_bias)


def per_device(
    inputs,
    segment_ids,
    gain_attn,
    w_qkv,
    w_out,
    gain_mlp,
    w_up,
    w_down,
    gain_final,
    head_projection_weight,
    head_output_bias,
    cotangent,
):
    core = lax.axis_index("head")
    place = lax.axis_index("dp")
    size = lax.axis_size("dp")
    rows, sequence_span = segment_ids.shape
    count, width = inputs.shape
    hdim = width // HEADS
    scale = 1.0 / math.sqrt(hdim)
    share = width // (2 * size)
    fused = size == HEADS and lax.axis_size("head") == 2 and rows == 1

    if fused:
        half = width // 2
        turn = hdim // 2
        freq = np.float32(10000.0) ** (-np.arange(turn, dtype=np.float32) / np.float32(turn))
        angle = np.arange(sequence_span, dtype=np.float32)[None, :] * freq[:, None]
        cosine_t, sine_t = jnp.asarray(np.cos(angle)), jnp.asarray(np.sin(angle))
        (
            y_t,
            g_t,
            a2_t,
            o_t,
            a1_t,
            y_o,
            g_o,
            a2_o,
            o_o,
            a1_o,
            dx3_t,
            e3_t,
            gain_columns,
            x2_t,
            x_t,
            h_t,
            qkv_t,
            lse,
        ) = run_forward(
            inputs,
            w_qkv,
            w_out,
            w_up,
            w_down,
            head_projection_weight,
            cotangent,
            segment_ids,
            [gain_attn, gain_mlp, gain_final],
            cosine_t,
            sine_t,
        )
        head, down, up, out, qkv, sums, entry = run_backward(
            [y_t, g_t, a2_t, o_t, a1_t],
            [y_o, g_o, a2_o, o_o, a1_o],
            [cotangent, dx3_t, e3_t, x2_t, x_t, h_t, qkv_t, gain_columns],
            [w_down, w_up, w_out, w_qkv],
            [lse, segment_ids, cosine_t, sine_t],
        )
        (
            entry_sensitivity_matrix,
            grad_head,
            grad_down,
            grad_up,
            grad_out,
            grad_qkv,
            predicted_levels,
            *gains,
            grad_bias,
        ) = run_finish(
            [entry, head, down, up, out, qkv],
            sums,
            y_t,
            y_o,
            head_projection_weight,
            head_output_bias,
        )
    else:
        other_rows = lax.dynamic_slice_in_dim(cotangent, (1 - core) * count, count, 0)
        own_rows = lax.dynamic_slice_in_dim(cotangent, core * count, count, 0)
        got = swap_cores(contract_cols(head_projection_weight, other_rows).astype(BF16))
        grad_final_t = contract_cols(head_projection_weight, own_rows) + got.astype(F32)
        bias_local = jnp.sum(cotangent, axis=0, dtype=F32)

        cosine, sine = rotary_tables(sequence_span, hdim)
        tokens = inputs.astype(jnp.float32)
        normed_one, inverse_one = rms_forward(tokens, gain_attn)
        act_one = normed_one.astype(jnp.bfloat16)
        projected = jnp.dot(act_one, w_qkv, preferred_element_type=jnp.float32).reshape(
            rows, sequence_span, 3, HEADS, hdim
        )
        query = rotate(projected[:, :, 0], cosine, sine).astype(jnp.bfloat16)
        key = rotate(projected[:, :, 1], cosine, sine).astype(jnp.bfloat16)
        value = projected[:, :, 2].astype(jnp.bfloat16)
        attended, log_total = lax.map(
            lambda items: attend_forward(items, scale), (query, key, value, segment_ids)
        )
        mixed = attended.reshape(rows * sequence_span, width)
        resid_two = tokens + jnp.dot(mixed, w_out, preferred_element_type=jnp.float32)
        normed_two, inverse_two = rms_forward(resid_two, gain_mlp)
        act_two = normed_two.astype(jnp.bfloat16)
        hidden_pre = jnp.dot(act_two, w_up, preferred_element_type=jnp.float32)
        hidden = jax.nn.silu(hidden_pre).astype(jnp.bfloat16)
        resid_three = resid_two + jnp.dot(hidden, w_down, preferred_element_type=jnp.float32)
        normed_three, inverse_three = rms_forward(resid_three, gain_final)
        final_hidden = normed_three.astype(jnp.bfloat16)
        other_hidden = swap_cores(final_hidden)
        collected_rows = jnp.concatenate(
            [
                jnp.where(core == 0, final_hidden, other_hidden),
                jnp.where(core == 0, other_hidden, final_hidden),
            ],
            axis=0,
        )
        predicted_levels = (
            jnp.dot(collected_rows, head_projection_weight, preferred_element_type=jnp.float32)
            + head_output_bias
        )
        grad_head = lax.psum_scatter(
            contract_rows(collected_rows, cotangent), "dp", scatter_dimension=0, tiled=True
        )
        grad_three, grad_gain_final = rms_backward(
            resid_three, inverse_three, gain_final, grad_final_t.T
        )
        grad_mlp_out = grad_three.astype(jnp.bfloat16)
        grad_hidden = contract_cols(grad_mlp_out, w_down)
        sigmoid = jax.nn.sigmoid(hidden_pre)
        grad_pre = (grad_hidden * sigmoid * (1.0 + hidden_pre * (1.0 - sigmoid))).astype(BF16)
        grad_norm_two, grad_gain_mlp = rms_backward(
            resid_two, inverse_two, gain_mlp, contract_cols(grad_pre, w_up)
        )
        grad_two = grad_three + grad_norm_two
        grad_branch = grad_two.astype(jnp.bfloat16)
        grad_mixed = (
            contract_cols(grad_branch, w_out)
            .astype(jnp.bfloat16)
            .reshape(rows, sequence_span, HEADS, hdim)
        )
        grad_query, grad_key, grad_value = lax.map(
            lambda items: attend_backward(items, scale),
            (query, key, value, segment_ids, log_total, grad_mixed),
        )
        grad_query = unrotate(grad_query, cosine, sine)
        grad_key = unrotate(grad_key, cosine, sine)
        grad_proj = (
            jnp.stack([grad_query, grad_key, grad_value], axis=2)
            .reshape(rows * sequence_span, 3 * width)
            .astype(jnp.bfloat16)
        )
        grad_norm_one, grad_gain_attn = rms_backward(
            tokens, inverse_one, gain_attn, contract_cols(grad_proj, w_qkv)
        )
        entry_sensitivity_matrix = grad_two + grad_norm_one
        grad_down = scatter_rows(hidden, grad_mlp_out)
        grad_up = scatter_rows(act_two, grad_pre)
        grad_out = scatter_rows(mixed, grad_branch)
        grad_qkv = scatter_rows(act_one, grad_proj)
        gains = sum_everywhere(jnp.stack([grad_gain_attn, grad_gain_mlp, grad_gain_final]), True)
        gains = lax.dynamic_slice_in_dim(gains, (place * 2 + core) * share, share, 1)
        grad_bias = sum_everywhere(bias_local, False)
    return (
        predicted_levels,
        entry_sensitivity_matrix,
        gains[0],
        grad_qkv,
        grad_out,
        gains[1],
        grad_up,
        grad_down,
        gains[2],
        grad_head,
        grad_bias,
    )


def solution(mesh):
    return jax.shard_map(
        per_device,
        mesh=mesh,
        in_specs=(
            P(("dp", "head"), None),
            P(("dp", "head"), None),
            P(),
            P(),
            P(),
            P(),
            P(),
            P(),
            P(),
            P(None, "head"),
            P("head"),
            P("dp", "head"),
        ),
        out_specs=(
            P("dp", "head"),
            P(("dp", "head"), None),
            P(("dp", "head")),
            P(("dp", "head"), None),
            P(("dp", "head"), None),
            P(("dp", "head")),
            P(("dp", "head"), None),
            P(("dp", "head"), None),
            P(("dp", "head")),
            P("dp", "head"),
            P("head"),
        ),
        check_vma=False,
    )
```

profile of v0, /device:TPU:0, one launch (start us, length us, event | category | flops | bytes accessed | tf_op | source)
XLA Modules:
  0.0 251.5 jit_solution(5974555368234786681)
XLA Ops:
  0.6 54.2 %forward.1 = (bf16[1280,512]{1,0:T(8,128)(2,1)}, bf16[5120,512]{1,0:T(8,128)(2,1)}, bf16[1280,512]{1,0:T(8,128)(2,1)}, bf16[1280,512]{1,0:T(8,128)(2,1)}, bf16[1...) custom-call(bf16[512,1280]{1,0:T(8,128)(2,1)} %x.1, ...), custom_call_target="tpu_custom_call" | custom-call | tf_op jit(solution)/shard_map/forward/pallas_call | solution.py:567
  54.8 187.8 %backward.1 = (f32[80,640]{1,0:T(8,128)}, f32[160,1280]{1,0:T(8,128)}, f32[40,5120]{1,0:T(8,128)}, f32[40,1280]{1,0:T(8,128)}, f32[40,3840]{1,0:T(8,128)}, /*ind...) custom-call(bf16[16,80,512]{2,1,0:T(8,128)(2,1)} %bitcast.12, ...), custom_call_target="tpu_custom_call" | custom-call | tf_op jit(solution)/shard_map/backward/pallas_call | solution.py:1542
  242.6 8.7 %finish.1 = (f32[512,1280]{1,0:T(8,128)}, f32[80,640]{1,0:T(8,128)}, f32[160,1280]{1,0:T(8,128)}, f32[40,5120]{1,0:T(8,128)}, f32[40,1280]{1,0:T(8,128)}, /*inde...) custom-call(f32[512,1280]{1,0:T(8,128)} %get-tuple-element.65.refs_0, ...), custom_call_target="tpu_custom_call" | custom-call | tf_op jit(solution)/shard_map/finish/pallas_call | solution.py:1694
where the time goes:
time: 252 us
  Pallas kernels  251 us (100%)
    pallas_call x1, Pallas kernels, run_backward(): pl.pallas_call(functools.partial(backward_kernel, table, size), out_shape...  188 us
    pallas_call x1, Pallas kernels, run_forward(): pl.pallas_call(forward_kernel, out_shape=shapes, in_specs=[hbm] * 7 + [vm...  54.2 us
    pallas_call x1, Pallas kernels, run_finish(): pl.pallas_call(functools.partial(finish_kernel, len(copied)), out_shape=s...  8.74 us

commit v1 on v0

--- a/solution.py
+++ b/solution.py
@@ -229,8 +229,6 @@
     w_out,
     w_up,
     w_down,
-    w_head,
-    cot,
     seg_row,
     gain_attn,
     gain_mlp,
@@ -242,13 +240,11 @@
     a2_t,
     o_t,
     a1_t,
-    y_o,
     g_o,
     a2_o,
     o_o,
     a1_o,
-    dx3_t,
-    e3_t,
+    x3_t,
     gain_columns,
     x2_t,
     x_t,
@@ -270,15 +266,8 @@
     bias,
     gains,
     gain_rows,
-    cbuf,
-    head_weight,
-    dy,
-    dy_sent,
-    dy_got,
-    e3,
     weight_sem,
     in_sem,
-    c_sem,
     out_sem,
     h_sem,
     g_sem,
@@ -323,21 +312,10 @@
             device_id_type=MESH,
         )
 
-    fetch_head_weight = pltpu.make_async_copy(w_head, head_weight, c_sem.at[2])
-
-    def fetch_c(number, which):
-        start = pl.multiple_of(which * tokens, 16)
-        return pltpu.make_async_copy(
-            cot.at[pl.ds(start, tokens)], cbuf.at[number], c_sem.at[number]
-        )
-
     fetch_x = pltpu.make_async_copy(x, xin, in_sem)
     fetch_x.start()
     for k in range(SLOTS):
         fetch(k).start()
-    fetch_c(1, other).start()
-    fetch_head_weight.start()
-    fetch_c(0, core).start()
 
     barrier = pltpu.get_barrier_semaphore()
     pl.semaphore_signal(barrier, inc=1, device_id=(me, other), device_id_type=MESH)
@@ -348,8 +326,7 @@
     mask_of(seg_row, bias)
     fetch_x.wait()
     xt[...] = xin[...].T
-    dy_push = remote(dy_sent, dy_got, push_send.at[0], push_recv.at[0])
-    outs, pushes = [], [dy_push]
+    outs, pushes = [], []
 
     def put(source, target, also=None):
         copy = pltpu.make_async_copy(source, target, out_sem.at[len(outs)])
@@ -361,6 +338,7 @@
             pushes[-1].start()
 
     put(xt, x_t)
+    put(gains, gain_columns)
 
     def squares_of(ref):
         def step(k, total):
@@ -432,18 +410,6 @@
 
     put(mixed, o_t, o_o)
 
-    fetch_head_weight.wait()
-    fetch_c(1, other).wait()
-    for i in range(2):
-        rows = slice(i * half, (i + 1) * half)
-        dy_sent[rows] = nt(head_weight[rows], cbuf[1]).astype(BF16)
-    dy_push.start()
-    fetch_c(0, core).wait()
-    for i in range(2):
-        rows = slice(i * half, (i + 1) * half)
-        dy[rows] = nt(head_weight[rows], cbuf[0])
-
-
     fetch(3).wait()
     for lower in range(2):
         rows = slice(lower * half, (lower + 1) * half)
@@ -502,24 +468,9 @@
         def _():
             fetch_down(k + 2).start()
 
+    put(res3, x3_t)
     normalize(res3, 2, final)
-    put(final, y_t, y_o)
-
-    dy_push.wait_recv()
-
-    @pl.loop(0, width // STRIP)
-    def _(k):
-        rows = pl.ds(pl.multiple_of(k * STRIP, STRIP), STRIP)
-        dy[rows] = dy[rows] + dy_got[rows].astype(F32)
-
-    def emit(k, rows, value):
-        dy[rows] = value
-        e3[rows] = value.astype(BF16)
-
-    norm_backward(res3, dy, gains, 2, emit)
-    put(dy, dx3_t)
-    put(e3, e3_t)
-    put(gains, gain_columns)
+    put(final, y_t)
     for copy in outs:
         copy.wait()
     for k in range(max(0, pieces - 2), pieces):
@@ -528,12 +479,11 @@
         g_push(k).wait_send()
     for k in range(pieces):
         g_push(k).wait_recv()
-    dy_push.wait_send()
-    for push in pushes[1:]:
+    for push in pushes:
         push.wait()
 
 
-def run_forward(x, w_qkv, w_out, w_up, w_down, w_head, cot, segs, gains, cosine, sine):
+def run_forward(x, w_qkv, w_out, w_up, w_down, segs, gains, cosine, sine):
     tokens, width = x.shape
     hidden = w_up.shape[1]
     hdim = width // HEADS
@@ -548,13 +498,11 @@
             (flat, BF16),
             (flat, BF16),
             (flat, BF16),
-            (flat, BF16),
             ((hidden, tokens), BF16),
             (flat, BF16),
             (flat, BF16),
             (flat, BF16),
             (flat, F32),
-            (flat, BF16),
             ((width, 128), F32),
             (flat, F32),
             (flat, BF16),
@@ -567,8 +515,8 @@
     return pl.pallas_call(
         forward_kernel,
         out_shape=shapes,
-        in_specs=[hbm] * 7 + [vmem] * 6,
-        out_specs=[hbm] * 17 + [vmem],
+        in_specs=[hbm] * 5 + [vmem] * 6,
+        out_specs=[hbm] * 15 + [vmem],
         scratch_shapes=[
             pltpu.VMEM((SLOTS, width, width), BF16),
             pltpu.VMEM((tokens, width), BF16),
@@ -585,20 +533,13 @@
             pltpu.VMEM((tokens, tokens), F32),
             pltpu.VMEM((width, 128), F32),
             pltpu.VMEM((8, width), F32),
-            pltpu.VMEM((2, tokens, width // 2), BF16),
-            pltpu.VMEM((width, width // 2), BF16),
-            pltpu.VMEM(flat, F32),
-            pltpu.VMEM(flat, BF16),
-            pltpu.VMEM(flat, BF16),
-            pltpu.VMEM(flat, BF16),
             dma((SLOTS,)),
             dma(()),
-            dma((3,)),
-            dma((10,)),
+            dma((9,)),
             dma((2,)),
             dma((2,)),
-            dma((5,)),
-            dma((5,)),
+            dma((3,)),
+            dma((3,)),
             dma((2,)),
             dma((hidden // width,)),
         ],
@@ -606,7 +547,7 @@
             collective_id=1, has_side_effects=True, vmem_limit_bytes=60 << 20
         ),
         name="forward",
-    )(x, w_qkv, w_out, w_up, w_down, w_head, cot, segs, *gains, cosine, sine)
+    )(x, w_qkv, w_out, w_up, w_down, segs, *gains, cosine, sine)
 
 
 LEAD = 3
@@ -620,14 +561,14 @@
     a2_t,
     o_t,
     a1_t,
-    y_o,
     g_o,
     a2_o,
     o_o,
     a1_o,
+    y_flat,
     cot,
-    dx3_t,
-    e3_t,
+    w_head,
+    x3_t,
     x2_t,
     x_t,
     h_t,
@@ -639,6 +580,7 @@
     w_qkv,
     lse,
     seg_row,
+    head_bias,
     cosine,
     sine,
     out_head,
@@ -648,6 +590,7 @@
     out_qkv,
     out_small,
     out_entry,
+    out_levels,
     e3_o,
     eh_o,
     e2_o,
@@ -747,8 +690,8 @@
     ring_side, ring_in = side.shape[0], side1.shape[0]
     main = grad.shape[-1]
 
-    fetch_dx = pltpu.make_async_copy(dx3_t, dx, fetch_sem.at[0])
-    fetch_e3 = pltpu.make_async_copy(e3_t, ebuf, fetch_sem.at[1])
+    fetch_head_weight = pltpu.make_async_copy(w_head, wcols.at[0], fetch_sem.at[0])
+    fetch_x3 = pltpu.make_async_copy(x3_t, work, fetch_sem.at[1])
     fetch_gains = pltpu.make_async_copy(gain_columns, gains, fetch_sem.at[4])
     fetch_x2 = pltpu.make_async_copy(x2_t, work, fetch_sem.at[1])
     fetch_x = pltpu.make_async_copy(x_t, ebuf, fetch_sem.at[0])
@@ -760,7 +703,7 @@
         )
 
     lefts = (y_t, g_t, a2_t, o_t, a1_t)
-    left_others = (y_o, g_o, a2_o, o_o, a1_o)
+    left_others = (None, g_o, a2_o, o_o, a1_o)
     pieces = hidden // width
 
     def start_left(c):
@@ -771,13 +714,14 @@
                 source.at[:, lower, :], lbuf.at[c % 2, half], left_sem.at[c % 2, half]
             ).start()
 
-    fetch_e3.start()
-    start_left(0)
+    fetch_y = pltpu.make_async_copy(y_t, lbuf.at[0, 0], left_sem.at[0, 0])
+    fetch_y.start()
+    local_c(1, other).start()
+    fetch_head_weight.start()
     local_c(0, core).start()
-    local_c(1, other).start()
+    fetch_x3.start()
+    fetch_gains.start()
     start_left(1)
-    fetch_dx.start()
-    fetch_gains.start()
 
     barrier = pltpu.get_barrier_semaphore()
     for index, which in ((me, other), (flip_x, core), (flip_y, core), (far, core)):
@@ -804,10 +748,14 @@
             device_id_type=MESH,
         )
 
-    PE3, PE2, PEP = range(3)
+    PE3, PE2, PEP, PY, PDY, PLEVEL = range(6)
 
     def push(k):
-        if k == PEP:
+        if k == PY:
+            src, dst = lbuf.at[0, 0], lbuf.at[0, 1]
+        elif k in (PDY, PLEVEL):
+            src, dst = ehbuf, hbuf
+        elif k == PEP:
             wide = 3 * cols
             src, dst = ep.at[pl.ds(pl.multiple_of(other * wide, 16), wide)], ep_o
         else:
@@ -815,8 +763,14 @@
             src = src.at[pl.ds(pl.multiple_of(other * cols, 16), cols)]
         return remote(src, dst, push_send.at[k], push_recv.at[k], me, other)
 
-    fetch_e3.wait()
-    push(PE3).start()
+    fetch_y.wait()
+    push(PY).start()
+    fetch_head_weight.wait()
+    local_c(1, other).wait()
+    for i in range(2):
+        ehbuf[i] = nt(wcols[0, i * cols : (i + 1) * cols], cbuf[1]).astype(BF16)
+    push(PDY).start()
+    local_c(0, core).wait()
 
     def start_right(c):
         i, j = table[c]
@@ -834,7 +788,6 @@
                     eh_push(piece, 0).wait_recv()
         elif i == 3:
             own, its = ebuf.at[mine], e2_o
-            push(PE2).wait_recv()
         else:
             start = pl.multiple_of(core * 3 * cols + j * cols, 16)
             own, its = ep.at[pl.ds(start, cols)], ep_o.at[rows]
@@ -1181,26 +1134,36 @@
                         def _():
                             start_results(d)
 
-    local_c(0, core).wait()
-    local_c(1, other).wait()
-    wait_left(0)
+    push(PY).wait_recv()
     form(0, [cbuf[0], cbuf[1]], nn)
+    push(PY).wait_send()
     start_left(2)
+
+    def emit_final(k, rows, value):
+        dx[rows] = value
+        ebuf[rows] = value.astype(BF16)
+
+    push(PDY).wait_recv()
+    for i in range(2):
+        rows = slice(i * cols, (i + 1) * cols)
+        dx[rows] = nt(wcols[0, rows], cbuf[0]) + hbuf[i].astype(F32)
+    fetch_x3.wait()
+    fetch_gains.wait()
+    norm_backward(work, dx, gains, 2, emit_final)
+    push(PE3).start()
     fetch_x2.start()
     sums[0] = jnp.zeros_like(sums[0])
     for i in range(2):
         share = jnp.sum(cbuf[i].astype(F32), axis=0, keepdims=True)
         at = pl.ds(pl.multiple_of(core * cols, 128), cols)
         sums[0, 3:4, at] = sums[0, 3:4, at] + share
+    push(PDY).wait_send()
     for c in range(1, LEAD):
         start_right(c)
         wait_left(c % 2)
         wait_right(c % 2)
         form(c, [rbuf[c % 2, 0], rbuf[c % 2, 1]], nt)
         start_left(c + 2)
-    fetch_dx.wait()
-    fetch_gains.wait()
-
     def row_tile(k, slot, source):
         return pltpu.make_async_copy(
             source.at[pl.ds(pl.multiple_of(k * cols, 16), cols)], wrows.at[slot], row_sem.at[slot]
@@ -1312,6 +1275,32 @@
             eo[pl.ds(k * group, group)] = value.reshape(group, hdim, tokens)
 
         mask_of(seg_row, bias)
+        pltpu.make_async_copy(w_head, wcols.at[0], col_sem.at[0]).start()
+        pltpu.make_async_copy(y_flat, ehbuf, h_sem.at[0]).start()
+
+    def level_copy(k, which, slot):
+        return pltpu.make_async_copy(
+            obuf.at[slot],
+            out_levels.at[
+                pl.ds(pl.multiple_of(which * tokens, 8), tokens), k * STRIP : (k + 1) * STRIP
+            ],
+            entry_sem.at[slot],
+        )
+
+    def levels(source, which):
+        last = cols // STRIP
+        for k in range(last):
+            if k >= 2:
+                level_copy(k - 2, which, k % 2).wait()
+            part = slice(k * STRIP, (k + 1) * STRIP)
+            obuf[k % 2] = (
+                tt(source[0], wcols[0, :cols, part])
+                + tt(source[1], wcols[0, cols:, part])
+                + head_bias[...].reshape(1, cols)[:, part]
+            )
+            level_copy(k, which, k % 2).start()
+        for k in range(last - 2, last):
+            level_copy(k, which, k % 2).wait()
 
     per_turn = count // 4
 
@@ -1433,10 +1422,34 @@
     @pl.loop(0, n + length)
     def _(t):
         for c in range(LEAD, n):
-
-            @pl.when(t == c - LEAD)
-            def _():
-                start_right(c)
+            if table[c] != (4, 0):
+
+                @pl.when(t == c - LEAD)
+                def _():
+                    start_right(c)
+
+        exchange(t)
+
+        for c in range(LEAD, n):
+            if table[c] == (4, 0):
+
+                @pl.when(t == c - LEAD)
+                def _():
+                    start_right(c)
+
+        @pl.when(t + LEAD < n)
+        def _():
+            c = t + LEAD
+            slot = lax.rem(c, 2)
+            wait_left(slot)
+            wait_right(slot)
+            send1(t).wait_send()
+            form(c, [rbuf[slot, 0], rbuf[slot, 1]], nt)
+            for d in range(LEAD + 2, n):
+
+                @pl.when(c == d - 2)
+                def _():
+                    start_left(d)
 
         @pl.when(t < 2)
         def _():
@@ -1451,6 +1464,22 @@
         @pl.when((t >= 3) & (t < 7))
         def _():
             attend(t - 3)
+
+        @pl.when(t == 3)
+        def _():
+            push(PE2).wait_recv()
+            pltpu.make_async_copy(y_flat, ehbuf, h_sem.at[0]).wait()
+            push(PLEVEL).start()
+
+        @pl.when(t == 4)
+        def _():
+            pltpu.make_async_copy(w_head, wcols.at[0], col_sem.at[0]).wait()
+            levels(ehbuf, core)
+
+        @pl.when(t == 5)
+        def _():
+            push(PLEVEL).wait()
+            levels(hbuf, other)
 
         @pl.when(t == 6)
         def _():
@@ -1478,22 +1507,6 @@
                 else:
                     sums[i + 1] = value
                     small_copy(i + 1).start()
-
-        exchange(t)
-
-        @pl.when(t + LEAD < n)
-        def _():
-            c = t + LEAD
-            slot = lax.rem(c, 2)
-            wait_left(slot)
-            wait_right(slot)
-            send1(t).wait_send()
-            form(c, [rbuf[slot, 0], rbuf[slot, 1]], nt)
-            for d in range(LEAD + 2, n):
-
-                @pl.when(c == d - 2)
-                def _():
-                    start_left(d)
 
         @pl.when(t == 8)
         def _():
@@ -1522,6 +1535,7 @@
     hdim = width // HEADS
     hbm = pl.BlockSpec(memory_space=pl.ANY)
     vmem = pl.BlockSpec(memory_space=pltpu.VMEM)
+    y_flat = lefts[0].reshape(2, cols, tokens)
     lefts = [left.reshape(size, left.shape[0] // size, tokens) for left in lefts + left_others]
     shapes = [
         jax.ShapeDtypeStruct((block, cols), F32),
@@ -1531,6 +1545,7 @@
         jax.ShapeDtypeStruct((share, 3 * width), F32),
         jax.ShapeDtypeStruct((8, width), F32),
         jax.ShapeDtypeStruct((tokens, width), F32),
+        jax.ShapeDtypeStruct((2 * tokens, cols), F32),
     ]
     shapes += [
         jax.ShapeDtypeStruct((rows, tokens), BF16)
@@ -1542,8 +1557,8 @@
     results = pl.pallas_call(
         functools.partial(backward_kernel, table, size),
         out_shape=shapes,
-        in_specs=[hbm] * 22 + [vmem] * 4,
-        out_specs=[hbm] * 5 + [vmem] + [hbm] * 6,
+        in_specs=[hbm] * 22 + [vmem] * 5,
+        out_specs=[hbm] * 5 + [vmem] + [hbm] * 7,
         scratch_shapes=[
             pltpu.VMEM((2, 2, size, block, tokens), BF16),
             pltpu.VMEM((2, 2, cols, tokens), BF16),
@@ -1577,8 +1592,8 @@
             pltpu.VMEM((HEADS, hdim, tokens), BF16),
             pltpu.VMEM((2, TOGETHER, 3, hdim, tokens), BF16),
             pltpu.VMEM((2, tokens, 128), F32),
-            dma((3,)),
-            dma((3,)),
+            dma((6,)),
+            dma((6,)),
             dma((2, 2)),
             dma((2, 2)),
             dma((LEAD,)),
@@ -1615,33 +1630,20 @@
             collective_id=0, has_side_effects=True, vmem_limit_bytes=62 << 20
         ),
         name="backward",
-    )(*lefts, *others, *weights, *tables)
-    return results[:7]
-
-
-def finish_kernel(
-    copied,
-    *refs,
-):
-    sources = refs[:copied]
-    sums, y_t, y_o, w_head, head_bias = refs[copied : copied + 5]
-    results = refs[copied + 5 :]
-    targets = results[:copied]
-    levels, gain_attn, gain_mlp, gain_final, bias = results[copied : copied + 5]
-    ybuf, wbuf, out, fetch_sem, copy_sem, in_sem, out_sem = results[copied + 5 : copied + 12]
-    held = results[copied + 12 :]
+    )(*lefts, y_flat, *others, *weights, *tables)
+    return results[:8]
+
+
+def finish_kernel(copied, *refs):
+    sources, sums = refs[:copied], refs[copied]
+    targets = refs[copied + 1 : 2 * copied + 1]
+    gain_attn, gain_mlp, gain_final, bias = refs[2 * copied + 1 : 2 * copied + 5]
+    held = refs[2 * copied + 5 : 3 * copied + 5]
+    fetch_sem, copy_sem = refs[3 * copied + 5 :]
     me = lax.axis_index("dp")
     core = lax.axis_index("head")
-    width, tokens = y_t.shape
-    half = width // 2
-    fetches = [
-        pltpu.make_async_copy(source, target, in_sem.at[i])
-        for i, (source, target) in enumerate(
-            ((w_head, wbuf), (y_t, ybuf.at[0]), (y_o, ybuf.at[1]))
-        )
-    ]
-    for fetch in fetches:
-        fetch.start()
+    width = sums.shape[1]
+    share, half = gain_attn.shape[0], bias.shape[0]
     arrivals = [
         pltpu.make_async_copy(source, buffer, fetch_sem.at[i])
         for i, (source, buffer) in enumerate(zip(sources, held))
@@ -1652,63 +1654,37 @@
     ]
     for arrival in arrivals:
         arrival.start()
-    share = gain_attn.shape[0]
     start = (me * 2 + core) * share
     rolled = pltpu.roll(sums[...], lax.rem(width - start, width), 1)
     for i, target in enumerate((gain_attn, gain_mlp, gain_final)):
         target[...] = rolled[i, :share]
     bias[...] = sums[3, pl.ds(pl.multiple_of(core * half, 128), half)]
-    fetches[0].wait()
-    part = tokens // 2
-
-    def level_copy(i):
-        which = core if i < 2 else 1 - core
-        start = pl.multiple_of(which * tokens + (i % 2) * part, 8)
-        return pltpu.make_async_copy(out.at[i], levels.at[pl.ds(start, part)], out_sem.at[i])
-
-    for i in range(4):
-        if i % 2 == 0:
-            fetches[1 + i // 2].wait()
-        at = slice((i % 2) * part, (i % 2 + 1) * part)
-        out[i] = tt(ybuf[i // 2, :, at], wbuf[...]) + head_bias[...].reshape(1, half)
-        level_copy(i).start()
-        for k in range(i * len(copies) // 4, (i + 1) * len(copies) // 4):
-            arrivals[k].wait()
-            copies[k].start()
-    for i in range(4):
-        level_copy(i).wait()
+    for arrival, copy in zip(arrivals, copies):
+        arrival.wait()
+        copy.start()
     for copy in copies:
         copy.wait()
 
 
-def run_finish(copied, sums, y_t, y_o, w_head, head_bias):
-    width, tokens = y_t.shape
-    half = width // 2
+def run_finish(copied, sums):
+    width = sums.shape[1]
     share = width // (2 * lax.axis_size("dp"))
     hbm = pl.BlockSpec(memory_space=pl.ANY)
     vmem = pl.BlockSpec(memory_space=pltpu.VMEM)
     dma = pltpu.SemaphoreType.DMA
     shapes = [jax.ShapeDtypeStruct(value.shape, F32) for value in copied]
-    shapes += [jax.ShapeDtypeStruct((2 * tokens, half), F32)]
-    shapes += [jax.ShapeDtypeStruct((share,), F32)] * 3 + [jax.ShapeDtypeStruct((half,), F32)]
+    shapes += [jax.ShapeDtypeStruct((share,), F32)] * 3
+    shapes += [jax.ShapeDtypeStruct((width // 2,), F32)]
     return pl.pallas_call(
         functools.partial(finish_kernel, len(copied)),
         out_shape=shapes,
-        in_specs=[hbm] * len(copied) + [vmem] + [hbm] * 3 + [vmem],
-        out_specs=[hbm] * (len(copied) + 1) + [vmem] * 4,
-        scratch_shapes=[
-            pltpu.VMEM((2, width, tokens), BF16),
-            pltpu.VMEM((width, half), BF16),
-            pltpu.VMEM((4, tokens // 2, half), F32),
-            dma((len(copied),)),
-            dma((len(copied),)),
-            dma((3,)),
-            dma((4,)),
-        ]
-        + [pltpu.VMEM(value.shape, F32) for value in copied],
+        in_specs=[hbm] * len(copied) + [vmem],
+        out_specs=[hbm] * len(copied) + [vmem] * 4,
+        scratch_shapes=[pltpu.VMEM(value.shape, F32) for value in copied]
+        + [dma((len(copied),)), dma((len(copied),))],
         compiler_params=pltpu.CompilerParams(vmem_limit_bytes=60 << 20),
         name="finish",
-    )(*copied, sums, y_t, y_o, w_head, head_bias)
+    )(*copied, sums)
 
 
 def per_device(
@@ -1747,13 +1723,11 @@
             a2_t,
             o_t,
             a1_t,
-            y_o,
             g_o,
             a2_o,
             o_o,
             a1_o,
-            dx3_t,
-            e3_t,
+            x3_t,
             gain_columns,
             x2_t,
             x_t,
@@ -1766,38 +1740,38 @@
             w_out,
             w_up,
             w_down,
-            head_projection_weight,
-            cotangent,
             segment_ids,
             [gain_attn, gain_mlp, gain_final],
             cosine_t,
             sine_t,
         )
-        head, down, up, out, qkv, sums, entry = run_backward(
+        head, down, up, out, qkv, sums, entry, levels = run_backward(
             [y_t, g_t, a2_t, o_t, a1_t],
-            [y_o, g_o, a2_o, o_o, a1_o],
-            [cotangent, dx3_t, e3_t, x2_t, x_t, h_t, qkv_t, gain_columns],
+            [g_o, a2_o, o_o, a1_o],
+            [
+                cotangent,
+                head_projection_weight,
+                x3_t,
+                x2_t,
+                x_t,
+                h_t,
+                qkv_t,
+                gain_columns,
+            ],
             [w_down, w_up, w_out, w_qkv],
-            [lse, segment_ids, cosine_t, sine_t],
+            [lse, segment_ids, head_output_bias, cosine_t, sine_t],
         )
         (
+            predicted_levels,
             entry_sensitivity_matrix,
             grad_head,
             grad_down,
             grad_up,
             grad_out,
             grad_qkv,
-            predicted_levels,
             *gains,
             grad_bias,
-        ) = run_finish(
-            [entry, head, down, up, out, qkv],
-            sums,
-            y_t,
-            y_o,
-            head_projection_weight,
-            head_output_bias,
-        )
+        ) = run_finish([levels, entry, head, down, up, out, qkv], sums)
     else:
         other_rows = lax.dynamic_slice_in_dim(cotangent, (1 - core) * count, count, 0)
         own_rows = lax.dynamic_slice_in_dim(cotangent, core * count, count, 0)

time: 252 us -> 243 us (0.964)
  Pallas kernels: 251 us -> 242 us
    pallas_call x1, Pallas kernels: 54.2 us -> 46.8 us  [run_forward(): pl.pallas_call(forward_kernel, out_shape=shapes, in_specs=[hbm] * 5 + [vm...]
where the time goes in v1:
time: 243 us
  Pallas kernels  242 us (100%)
    pallas_call x1, Pallas kernels, run_backward(): pl.pallas_call(functools.partial(backward_kernel, table, size), out_shape...  188 us
    pallas_call x1, Pallas kernels, run_forward(): pl.pallas_call(forward_kernel, out_shape=shapes, in_specs=[hbm] * 5 + [vm...  46.8 us
    pallas_call x1, Pallas kernels, run_finish(): pl.pallas_call(functools.partial(finish_kernel, len(copied)), out_shape=s...  6.97 us

profile of v1, /device:TPU:0, one launch (start us, length us, event | category | flops | bytes accessed | tf_op | source)
XLA Modules:
  0.0 242.7 jit_solution(3402393938978769759)
XLA Ops:
  0.6 46.8 %forward.1 = (bf16[1280,512]{1,0:T(8,128)(2,1)}, bf16[5120,512]{1,0:T(8,128)(2,1)}, bf16[1280,512]{1,0:T(8,128)(2,1)}, bf16[1280,512]{1,0:T(8,128)(2,1)}, bf16[1...) custom-call(bf16[512,1280]{1,0:T(8,128)(2,1)} %x.1, ...), custom_call_target="tpu_custom_call" | custom-call | tf_op jit(solution)/shard_map/forward/pallas_call | solution.py:515
  47.5 188.0 %backward.1 = (f32[80,640]{1,0:T(8,128)}, f32[160,1280]{1,0:T(8,128)}, f32[40,5120]{1,0:T(8,128)}, f32[40,1280]{1,0:T(8,128)}, f32[40,3840]{1,0:T(8,128)}, /*ind...) custom-call(bf16[16,80,512]{2,1,0:T(8,128)(2,1)} %bitcast.12, ...), custom_call_target="tpu_custom_call" | custom-call | tf_op jit(solution)/shard_map/backward/pallas_call | solution.py:1557
  235.5 7.0 %finish.1 = (f32[1024,640]{1,0:T(8,128)}, f32[512,1280]{1,0:T(8,128)}, f32[80,640]{1,0:T(8,128)}, f32[160,1280]{1,0:T(8,128)}, f32[40,5120]{1,0:T(8,128)}, /*ind...) custom-call(f32[1024,640]{1,0:T(8,128)} %get-tuple-element.62.refs_0, ...), custom_call_target="tpu_custom_call" | custom-call | tf_op jit(solution)/shard_map/finish/pallas_call | solution.py:1678

commit v2 on v1

--- a/solution.py
+++ b/solution.py
@@ -403,10 +403,10 @@
             mixed[rows_of(0), asked] = nn(v_t[:, low:high], probs).astype(BF16)
             lse[head, :, asked] = peak + jnp.log(amount)
 
-    @pl.loop(0, count // TOGETHER)
+    @pl.loop(0, count // 4)
     def _(i):
-        for u in range(TOGETHER):
-            attend(i * TOGETHER + u)
+        for u in range(4):
+            attend(i * 4 + u)
 
     put(mixed, o_t, o_o)
 
@@ -450,7 +450,7 @@
             rows = slice(lower * half, (lower + 1) * half)
             value = tt(weights[up, :, rows], act2[...])
             hbuf[slot, rows] = value.astype(BF16)
-            gbuf[slot, rows] = (value / (1.0 + jnp.exp(-value))).astype(BF16)
+            gbuf[slot, rows] = (value * (0.5 * jnp.tanh(0.5 * value) + 0.5)).astype(BF16)
 
         @pl.when(k + 2 < pieces)
         def _():
@@ -783,11 +783,10 @@
                 push(PE3).wait_recv()
         elif i == 2:
             own, its = eh_mine.at[rows], eh_o.at[rows]
-            if j == 0:
-                for piece in range(pieces):
-                    eh_push(piece, 0).wait_recv()
+            eh_push(j).wait_recv()
         elif i == 3:
             own, its = ebuf.at[mine], e2_o
+            push(PE2).wait_recv()
         else:
             start = pl.multiple_of(core * 3 * cols + j * cols, 16)
             own, its = ep.at[pl.ds(start, cols)], ep_o.at[rows]
@@ -796,14 +795,21 @@
         pltpu.make_async_copy(own, rbuf.at[slot, 0], right_sem.at[slot, 0]).start()
         pltpu.make_async_copy(its, rbuf.at[slot, 1], right_sem.at[slot, 1]).start()
 
-    def eh_push(piece, slot):
+    def eh_push(piece):
         return remote(
-            ehbuf.at[slot],
-            eh_o.at[pl.ds(piece * cols, cols)],
-            eh_out_sem.at[slot],
+            ehbuf.at[0],
+            eh_o.at[pl.ds(pl.multiple_of(piece * cols, 16), cols)],
+            eh_out_sem.at[0],
             eh_in_sem.at[piece],
             me,
             other,
+        )
+
+    def eh_keep(piece):
+        return pltpu.make_async_copy(
+            ehbuf.at[1],
+            eh_mine.at[pl.ds(pl.multiple_of(piece * cols, 16), cols)],
+            eh_out_sem.at[1],
         )
 
     def wait_left(slot):
@@ -1056,6 +1062,8 @@
                 copy.wait()
 
     def exchange(t):
+        exchange_side(t)
+
         @pl.when(t < n)
         def _():
             c = t
@@ -1086,7 +1094,6 @@
 
             start_line(c, 1)
 
-        exchange_side(t)
 
         for step in range(1, length):
 
@@ -1182,7 +1189,7 @@
         )
 
     def mlp_tiles(k):
-        return jnp.where(k < pieces, other, core) * pieces + lax.rem(k, pieces)
+        return jnp.where(lax.rem(k, 2) == 0, other, core) * pieces + k // 2
 
     def fetch_mlp(k):
         slot = lax.rem(k, 2)
@@ -1197,37 +1204,29 @@
         row_tile(tile, slot, w_down).wait()
         h_tile(tile, slot).wait()
 
-        @pl.when((k >= 2) & (k < pieces + 2))
-        def _():
-            eh_push(0, slot).wait_send()
-
-        @pl.when(k >= pieces + 2)
-        def _():
-            pltpu.make_async_copy(
-                ehbuf.at[slot], eh_mine.at[pl.ds(0, cols)], eh_out_sem.at[slot]
-            ).wait()
+        @pl.when((k >= 2) & (slot == 0))
+        def _():
+            eh_push(0).wait_send()
+
+        @pl.when((k >= 2) & (slot == 1))
+        def _():
+            eh_keep(0).wait()
 
         part = cols // 2
         for i in range(2):
             rows = slice(i * part, (i + 1) * part)
             value = nn(wrows[slot, rows], ebuf[...])
             pre = hbuf[slot, rows].astype(F32)
-            sig = 1.0 / (1.0 + jnp.exp(-pre))
+            sig = 0.5 * jnp.tanh(0.5 * pre) + 0.5
             ehbuf[slot, rows] = (value * sig * (1.0 + pre * (1.0 - sig))).astype(BF16)
 
-        where = lax.rem(k, pieces)
-
-        @pl.when(k < pieces)
-        def _():
-            eh_push(where, slot).start()
-
-        @pl.when(k >= pieces)
-        def _():
-            pltpu.make_async_copy(
-                ehbuf.at[slot],
-                eh_mine.at[pl.ds(pl.multiple_of(where * cols, 16), cols)],
-                eh_out_sem.at[slot],
-            ).start()
+        @pl.when(slot == 0)
+        def _():
+            eh_push(k // 2).start()
+
+        @pl.when(slot == 1)
+        def _():
+            eh_keep(k // 2).start()
 
         col_tile(tile, slot, w_up).wait()
         accumulate(wcols.at[slot], ehbuf.at[slot], k == 0)
@@ -1255,10 +1254,8 @@
         ebuf[rows] = value.astype(BF16)
 
     def middle():
-        for slot in range(2):
-            pltpu.make_async_copy(
-                ehbuf.at[slot], eh_mine.at[pl.ds(0, cols)], eh_out_sem.at[slot]
-            ).wait()
+        eh_push(0).wait_send()
+        eh_keep(0).wait()
         row_tile(0, 0, w_out).start()
         row_tile(1, 1, w_out).start()
         push(PE3).wait_send()
@@ -1275,8 +1272,6 @@
             eo[pl.ds(k * group, group)] = value.reshape(group, hdim, tokens)
 
         mask_of(seg_row, bias)
-        pltpu.make_async_copy(w_head, wcols.at[0], col_sem.at[0]).start()
-        pltpu.make_async_copy(y_flat, ehbuf, h_sem.at[0]).start()
 
     def level_copy(k, which, slot):
         return pltpu.make_async_copy(
@@ -1302,7 +1297,8 @@
         for k in range(last - 2, last):
             level_copy(k, which, k % 2).wait()
 
-    per_turn = count // 4
+    pairs = count // TOGETHER
+    per_turn = -(-pairs // 3)
 
     def head_copy(head, slot, u, part):
         return pltpu.make_async_copy(
@@ -1354,9 +1350,8 @@
         def _():
             fetch_heads(0)
 
-        @pl.loop(0, per_turn // TOGETHER)
-        def _(j):
-            i = turn * (per_turn // TOGETHER) + j
+        @pl.loop(turn * per_turn, jnp.minimum((turn + 1) * per_turn, pairs))
+        def _(i):
             slot = lax.rem(i, 2)
             for u in range(TOGETHER):
                 for part in range(3):
@@ -1369,7 +1364,7 @@
             for u in range(TOGETHER):
                 attend_head(i * TOGETHER + u, slot, u)
 
-        @pl.when(turn == 3)
+        @pl.when(turn == 2)
         def _():
             push(PEP).start()
 
@@ -1451,35 +1446,19 @@
                 def _():
                     start_left(d)
 
-        @pl.when(t < 2)
-        def _():
-            @pl.loop(0, pieces)
-            def _(i):
-                mlp_step(t * pieces + i)
-
-        @pl.when(t == 2)
+        @pl.when(t < 3)
+        def _():
+            @pl.loop(t * 3, jnp.minimum(t * 3 + 3, 2 * pieces))
+            def _(k):
+                mlp_step(k)
+
+        @pl.when(t == 3)
         def _():
             middle()
 
-        @pl.when((t >= 3) & (t < 7))
-        def _():
-            attend(t - 3)
-
-        @pl.when(t == 3)
-        def _():
-            push(PE2).wait_recv()
-            pltpu.make_async_copy(y_flat, ehbuf, h_sem.at[0]).wait()
-            push(PLEVEL).start()
-
-        @pl.when(t == 4)
-        def _():
-            pltpu.make_async_copy(w_head, wcols.at[0], col_sem.at[0]).wait()
-            levels(ehbuf, core)
-
-        @pl.when(t == 5)
-        def _():
-            push(PLEVEL).wait()
-            levels(hbuf, other)
+        @pl.when((t >= 4) & (t < 7))
+        def _():
+            attend(t - 4)
 
         @pl.when(t == 6)
         def _():
@@ -1494,7 +1473,22 @@
 
         @pl.when(t == 9)
         def _():
+            pltpu.make_async_copy(w_head, wcols.at[0], col_sem.at[0]).start()
+            fetch_level = pltpu.make_async_copy(y_flat, ehbuf, h_sem.at[0])
+            fetch_level.start()
             last()
+            fetch_level.wait()
+            push(PLEVEL).start()
+
+        @pl.when(t == 10)
+        def _():
+            pltpu.make_async_copy(w_head, wcols.at[0], col_sem.at[0]).wait()
+            levels(ehbuf, core)
+
+        @pl.when(t == 11)
+        def _():
+            push(PLEVEL).wait()
+            levels(hbuf, other)
 
         for i in range(steps):
 

time: 243 us -> 239 us (0.984)
  Pallas kernels: 242 us -> 237 us
where the time goes in v2:
time: 239 us; the launch traced here: 238 us
  Pallas kernels  237 us (99%)
    pallas_call x1, Pallas kernels, run_backward(): pl.pallas_call(functools.partial(backward_kernel, table, size), out_shape...  186 us
    pallas_call x1, Pallas kernels, run_forward(): pl.pallas_call(forward_kernel, out_shape=shapes, in_specs=[hbm] * 5 + [vm...  44.5 us
    pallas_call x1, Pallas kernels, run_finish(): pl.pallas_call(functools.partial(finish_kernel, len(copied)), out_shape=s...  6.97 us

profile of v2, /device:TPU:0, one launch (start us, length us, event | category | flops | bytes accessed | tf_op | source)
XLA Modules:
  0.0 238.2 jit_solution(14194638815929954431)
XLA Ops:
  0.6 44.5 %forward.1 = (bf16[1280,512]{1,0:T(8,128)(2,1)}, bf16[5120,512]{1,0:T(8,128)(2,1)}, bf16[1280,512]{1,0:T(8,128)(2,1)}, bf16[1280,512]{1,0:T(8,128)(2,1)}, bf16[1...) custom-call(bf16[512,1280]{1,0:T(8,128)(2,1)} %x.1, ...), custom_call_target="tpu_custom_call" | custom-call | tf_op jit(solution)/shard_map/forward/pallas_call | solution.py:515
  45.1 185.9 %backward.1 = (f32[80,640]{1,0:T(8,128)}, f32[160,1280]{1,0:T(8,128)}, f32[40,5120]{1,0:T(8,128)}, f32[40,1280]{1,0:T(8,128)}, f32[40,3840]{1,0:T(8,128)}, /*ind...) custom-call(bf16[16,80,512]{2,1,0:T(8,128)(2,1)} %bitcast.12, ...), custom_call_target="tpu_custom_call" | custom-call | tf_op jit(solution)/shard_map/backward/pallas_call | solution.py:1551
  231.0 7.0 %finish.1 = (f32[1024,640]{1,0:T(8,128)}, f32[512,1280]{1,0:T(8,128)}, f32[80,640]{1,0:T(8,128)}, f32[160,1280]{1,0:T(8,128)}, f32[40,5120]{1,0:T(8,128)}, /*ind...) custom-call(f32[1024,640]{1,0:T(8,128)} %get-tuple-element.62.refs_0, ...), custom_call_target="tpu_custom_call" | custom-call | tf_op jit(solution)/shard_map/finish/pallas_call | solution.py:1672

commit v3 on v2

--- a/solution.py
+++ b/solution.py
@@ -1141,6 +1141,33 @@
                         def _():
                             start_results(d)
 
+    def row_tile(k, slot, source):
+        return pltpu.make_async_copy(
+            source.at[pl.ds(pl.multiple_of(k * cols, 16), cols)], wrows.at[slot], row_sem.at[slot]
+        )
+
+    def col_tile(k, slot, source):
+        return pltpu.make_async_copy(
+            source.at[:, pl.ds(pl.multiple_of(k * cols, 128), cols)],
+            wcols.at[slot],
+            col_sem.at[slot],
+        )
+
+    def h_tile(k, slot):
+        return pltpu.make_async_copy(
+            h_t.at[pl.ds(pl.multiple_of(k * cols, 16), cols)], hbuf.at[slot], h_sem.at[slot]
+        )
+
+    def mlp_tiles(k):
+        return jnp.where(lax.rem(k, 2) == 0, other, core) * pieces + k // 2
+
+    def fetch_mlp(k):
+        slot = lax.rem(k, 2)
+        tile = mlp_tiles(k)
+        row_tile(tile, slot, w_down).start()
+        col_tile(tile, slot, w_up).start()
+        h_tile(tile, slot).start()
+
     push(PY).wait_recv()
     form(0, [cbuf[0], cbuf[1]], nn)
     push(PY).wait_send()
@@ -1154,16 +1181,13 @@
     for i in range(2):
         rows = slice(i * cols, (i + 1) * cols)
         dx[rows] = nt(wcols[0, rows], cbuf[0]) + hbuf[i].astype(F32)
+    fetch_mlp(0)
+    fetch_mlp(1)
     fetch_x3.wait()
     fetch_gains.wait()
     norm_backward(work, dx, gains, 2, emit_final)
     push(PE3).start()
     fetch_x2.start()
-    sums[0] = jnp.zeros_like(sums[0])
-    for i in range(2):
-        share = jnp.sum(cbuf[i].astype(F32), axis=0, keepdims=True)
-        at = pl.ds(pl.multiple_of(core * cols, 128), cols)
-        sums[0, 3:4, at] = sums[0, 3:4, at] + share
     push(PDY).wait_send()
     for c in range(1, LEAD):
         start_right(c)
@@ -1171,33 +1195,6 @@
         wait_right(c % 2)
         form(c, [rbuf[c % 2, 0], rbuf[c % 2, 1]], nt)
         start_left(c + 2)
-    def row_tile(k, slot, source):
-        return pltpu.make_async_copy(
-            source.at[pl.ds(pl.multiple_of(k * cols, 16), cols)], wrows.at[slot], row_sem.at[slot]
-        )
-
-    def col_tile(k, slot, source):
-        return pltpu.make_async_copy(
-            source.at[:, pl.ds(pl.multiple_of(k * cols, 128), cols)],
-            wcols.at[slot],
-            col_sem.at[slot],
-        )
-
-    def h_tile(k, slot):
-        return pltpu.make_async_copy(
-            h_t.at[pl.ds(pl.multiple_of(k * cols, 16), cols)], hbuf.at[slot], h_sem.at[slot]
-        )
-
-    def mlp_tiles(k):
-        return jnp.where(lax.rem(k, 2) == 0, other, core) * pieces + k // 2
-
-    def fetch_mlp(k):
-        slot = lax.rem(k, 2)
-        tile = mlp_tiles(k)
-        row_tile(tile, slot, w_down).start()
-        col_tile(tile, slot, w_up).start()
-        h_tile(tile, slot).start()
-
     def mlp_step(k):
         slot = lax.rem(k, 2)
         tile = mlp_tiles(k)
@@ -1245,8 +1242,6 @@
             rows = slice(i * part, (i + 1) * part)
             acc[rows] += nn(left[rows], right[...])
 
-    fetch_mlp(0)
-    fetch_mlp(1)
 
     def emit_mlp(k, rows, value):
         value = dx[rows] + value
@@ -1464,6 +1459,11 @@
         def _():
             fetch_qkv(0)
             fetch_qkv(1)
+            sums[0] = jnp.zeros_like(sums[0])
+            for i in range(2):
+                share = jnp.sum(cbuf[i].astype(F32), axis=0, keepdims=True)
+                at = pl.ds(pl.multiple_of(core * cols, 128), cols)
+                sums[0, 3:4, at] = sums[0, 3:4, at] + share
 
         @pl.when((t == 7) | (t == 8))
         def _():

time: 239 us -> 239 us (level)
  no operation moved by 1% of the time
where the time goes in v3:
time: 239 us; the launch traced here: 238 us
  Pallas kernels  237 us (99%)
    pallas_call x1, Pallas kernels, run_backward(): pl.pallas_call(functools.partial(backward_kernel, table, size), out_shape...  186 us
    pallas_call x1, Pallas kernels, run_forward(): pl.pallas_call(forward_kernel, out_shape=shapes, in_specs=[hbm] * 5 + [vm...  44.5 us
    pallas_call x1, Pallas kernels, run_finish(): pl.pallas_call(functools.partial(finish_kernel, len(copied)), out_shape=s...  6.97 us

profile of v3, /device:TPU:0, one launch (start us, length us, event | category | flops | bytes accessed | tf_op | source)
XLA Modules:
  0.0 238.2 jit_solution(89471068095040017)
XLA Ops:
  0.6 44.5 %forward.1 = (bf16[1280,512]{1,0:T(8,128)(2,1)}, bf16[5120,512]{1,0:T(8,128)(2,1)}, bf16[1280,512]{1,0:T(8,128)(2,1)}, bf16[1280,512]{1,0:T(8,128)(2,1)}, bf16[1...) custom-call(bf16[512,1280]{1,0:T(8,128)(2,1)} %x.1, ...), custom_call_target="tpu_custom_call" | custom-call | tf_op jit(solution)/shard_map/forward/pallas_call | solution.py:515
  45.1 185.9 %backward.1 = (f32[80,640]{1,0:T(8,128)}, f32[160,1280]{1,0:T(8,128)}, f32[40,5120]{1,0:T(8,128)}, f32[40,1280]{1,0:T(8,128)}, f32[40,3840]{1,0:T(8,128)}, /*ind...) custom-call(bf16[16,80,512]{2,1,0:T(8,128)(2,1)} %bitcast.12, ...), custom_call_target="tpu_custom_call" | custom-call | tf_op jit(solution)/shard_map/backward/pallas_call | solution.py:1551
  231.0 7.0 %finish.1 = (f32[1024,640]{1,0:T(8,128)}, f32[512,1280]{1,0:T(8,128)}, f32[80,640]{1,0:T(8,128)}, f32[160,1280]{1,0:T(8,128)}, f32[40,5120]{1,0:T(8,128)}, /*ind...) custom-call(f32[1024,640]{1,0:T(8,128)} %get-tuple-element.62.refs_0, ...), custom_call_target="tpu_custom_call" | custom-call | tf_op jit(solution)/shard_map/finish/pallas_call | solution.py:1672
